TPU v7x, 512 devices: a whole 4x8x8 slice. The times are simulated.
512 devices in a mesh: row: 64 (over z, y), col: 8 (over x, core).
Axes of the slice: x: 4, y: 8, z: 8, core: 2. Of those that a mesh axis runs over, the one named last changes fastest.
Arguments:
- frames: bfloat16 [4, 16384, 8192], P(None, 'row', 'col'), may hold values from -6 to 6
- row_factor: bfloat16 [16384, 256], P('row')
- col_factor: bfloat16 [8192, 256], P('col')
- row_history: float32 [16384, 256], P('row'), may hold values from -8 to 8
- col_history: float32 [8192, 256], P('col'), may hold values from -8 to 8
- time_gram: float32 [256, 256], replicated, as said below
Outputs:
- frame_factor: float32 [4, 256], replicated
- new_row_factor: bfloat16 [16384, 256], P('row')
- new_col_factor: bfloat16 [8192, 256], P('col')
Inputs may be any that keep to these rules, and one draw needn't show every extreme that they name: `time_gram`: symmetric positive definite.
All inputs are finite; a program needn't handle non-finite values.
Results may differ from a plain program's by a relative error of at most 0.0041.
Values may be sent and summed in bfloat16 or wider, within the bound.
No kernel may reach another device: no remote copies, remote signals or barrier semaphores. Data moves between devices by JAX's collectives and lax.ppermute only.
A program may use at most 64 MiB of HBM per device.

v0:
```python
import jax
import jax.numpy as jnp
from jax import lax
from jax.sharding import PartitionSpec as P


def inner_gram(matrix):
    return lax.dot_general(
        matrix, matrix, (((0,), (0,)), ((), ())), preferred_element_type=jnp.float32
    )


def gram_solve(rhs, gram):
    lower_factor = jnp.linalg.cholesky(gram)
    return jax.scipy.linalg.cho_solve((lower_factor, True), rhs.T).T


def body(frames, row_factor, col_factor, row_history, col_history, time_gram):
    row_part = inner_gram(row_factor)
    col_part = inner_gram(col_factor)
    local_slab = jnp.einsum("bij,jr->bir", frames, col_factor, preferred_element_type=jnp.float32)
    slab_products, col_gram = lax.psum((local_slab, col_part), "col")
    rhs_part = jnp.sum(slab_products * row_factor.astype(jnp.float32)[None], axis=1)
    row_gram, frame_rhs = lax.psum((row_part, rhs_part), "row")
    frame_factor = gram_solve(frame_rhs, row_gram * col_gram)
    time_new = time_gram + jnp.dot(frame_factor.T, frame_factor, precision=lax.Precision.HIGHEST)
    row_sums = row_history + jnp.sum(frame_factor[:, None, :] * slab_products, axis=0)
    new_row = gram_solve(row_sums, time_new * col_gram).astype(jnp.bfloat16)
    new_gram_part = inner_gram(new_row)
    products = jnp.einsum("bij,ir->bjr", frames, new_row, preferred_element_type=jnp.float32)
    col_total, new_row_gram = lax.psum(
        (jnp.sum(frame_factor[:, None, :] * products, axis=0), new_gram_part), "row"
    )
    new_col = gram_solve(col_history + col_total, time_new * new_row_gram).astype(jnp.bfloat16)
    return (frame_factor, new_row, new_col)


def solution(mesh):
    in_specs = (
        P(None, "row", "col"),
        P("row", None),
        P("col", None),
        P("row", None),
        P("col", None),
        P(),
    )
    out_specs = (P(), P("row", None), P("col", None))
    return jax.shard_map(body, mesh=mesh, in_specs=in_specs, out_specs=out_specs, check_vma=False)
```

profile of v0, /device:TPU:6, one launch (start us, length us, event | category | flops | bytes accessed | tf_op | source)
XLA Modules:
  0.0 763.9 jit_solution(165622467089967468)
XLA Ops:
  7.2 2.0 fusion.47
  9.3 2.8 fusion.3
  14.9 153.5 %all-reduce.7.cloned.1.call-done = f32[256,256]{0,1:T(8,128)} async-done(((f32[256,256]{0,1:T(8,128)}), f32[256,256]{0,1:T(8,128)}) %all-reduce.7.cloned.1.call-update) | async-done | bytes 262160 | tf_op jit(solution)/shard_map/psum | solution.py:24
  168.4 70.8 %all-reduce.11.cloned.1.call-done = (f32[256,256]{0,1:T(8,128)}, f32[4,256,256]{2,1,0:T(8,128)}) async-done(((f32[256,256]{0,1:T(8,128)}, f32[4,256,256]{2,1,0:T(8,128)}), (f32[256,256]{0,1:T(8,128)}, f32[4,256,256]{2,1,0:T(8,128)})) %all-reduce.11.cloned.1.call-update) | async-done | bytes 1310736 | tf_op jit(solution)/shard_map/psum | solution.py:22
  242.8 11.7 %cholesky.172 = f32[128,128]{1,0:T(8,128)S(1)} custom-call(f32[128,128]{1,0:T(8,128)S(1)} %cholesky.270), custom_call_target="Cholesky" | custom-call | tf_op jit(solution)/shard_map/jit(cholesky)/cholesky | solution.py:14
  254.5 9.8 %custom-call.34 = f32[1,128,128]{1,2,0:T(8,128)S(1)} custom-call(f32[1,128,128]{2,1,0:T(8,128)S(1)} %get-tuple-element.79), custom_call_target="InvertDiagBlocksLowerTriangular" | custom-call | tf_op jit(solution)/shard_map/jit(cholesky)/cholesky | solution.py:14
  266.5 11.7 %cholesky.189 = f32[128,128]{1,0:T(8,128)S(1)} custom-call(f32[128,128]{1,0:T(8,128)S(1)} %convolution_subtract_fusion.6), custom_call_target="Cholesky" | custom-call | tf_op jit(solution)/shard_map/jit(cholesky)/cholesky | solution.py:14
  281.2 4.2 while.3
  282.0 1.4 bitcast_dynamic-update-slice_fusion.6
  284.0 1.4 bitcast_dynamic-update-slice_fusion.6
  286.1 20.5 %custom-call.29 = f32[2,128,128]{1,2,0:T(8,128)S(1)} custom-call(f32[2,128,128]{2,1,0:T(8,128)} %copy-done.13), custom_call_target="InvertDiagBlocksLowerTriangular" | custom-call | tf_op jit(solution)/shard_map/jit(_cho_solve)/triangular_solve | solution.py:15
  307.6 144.2 %psum.45 = f32[256,4]{0,1:T(4,128)S(1)} all-reduce(f32[256,4]{0,1:T(4,128)S(1)} %bitcast.139), channel_id=1, replica_groups=mesh['row'=64,'col'=8] {'row'}, use_global_device_ids=true, to_apply=%region_8.10 | all-reduce | flops 1024 | bytes 8192 | tf_op jit(solution)/shard_map/psum | solution.py:24
  453.2 2.2 fusion.44
  457.8 11.7 %cholesky.206 = f32[128,128]{1,0:T(8,128)S(1)} custom-call(f32[128,128]{1,0:T(8,128)S(1)} %cholesky.273), custom_call_target="Cholesky" | custom-call | tf_op jit(solution)/shard_map/jit(cholesky)/cholesky | solution.py:14
  469.6 9.8 %custom-call.35 = f32[1,128,128]{1,2,0:T(8,128)S(1)} custom-call(f32[1,128,128]{2,1,0:T(8,128)S(1)} %get-tuple-element.75), custom_call_target="InvertDiagBlocksLowerTriangular" | custom-call | tf_op jit(solution)/shard_map/jit(cholesky)/cholesky | solution.py:14
  481.6 11.7 %cholesky.223 = f32[128,128]{1,0:T(8,128)S(1)} custom-call(f32[128,128]{1,0:T(8,128)S(1)} %convolution_subtract_fusion.5), custom_call_target="Cholesky" | custom-call | tf_op jit(solution)/shard_map/jit(cholesky)/cholesky | solution.py:14
  497.0 4.1 while.4
  497.6 1.4 bitcast_dynamic-update-slice_fusion.7
  499.6 1.4 bitcast_dynamic-update-slice_fusion.7
  501.7 20.7 %custom-call.30 = f32[2,128,128]{1,2,0:T(8,128)S(1)} custom-call(f32[2,128,128]{2,1,0:T(8,128)} %copy-done.14), custom_call_target="InvertDiagBlocksLowerTriangular" | custom-call | tf_op jit(solution)/shard_map/jit(_cho_solve)/triangular_solve | solution.py:15
  528.0 1.8 fusion
  529.8 1.6 copy.27
  532.2 150.4 %all-reduce.9.cloned.1.call-done = (f32[1024,256]{0,1:T(8,128)}, f32[256,256]{0,1:T(8,128)}) async-done(((f32[1024,256]{0,1:T(8,128)}, f32[256,256]{0,1:T(8,128)}), (f32[1024,256]{0,1:T(8,128)}, f32[256,256]{0,1:T(8,128)})) %all-reduce.9.cloned.1.call-update) | async-done | bytes 1310736 | tf_op jit(solution)/shard_map/psum | solution.py:31
  686.2 11.7 %cholesky.240 = f32[128,128]{1,0:T(8,128)S(1)} custom-call(f32[128,128]{1,0:T(8,128)S(1)} %cholesky.276), custom_call_target="Cholesky" | custom-call | tf_op jit(solution)/shard_map/jit(cholesky)/cholesky | solution.py:14
  698.0 9.8 %custom-call.36 = f32[1,128,128]{1,2,0:T(8,128)S(1)} custom-call(f32[1,128,128]{2,1,0:T(8,128)S(1)} %get-tuple-element.71), custom_call_target="InvertDiagBlocksLowerTriangular" | custom-call | tf_op jit(solution)/shard_map/jit(cholesky)/cholesky | solution.py:14
  708.9 1.1 convolution_subtract_fusion.4
  710.0 11.9 %cholesky.257 = f32[128,128]{1,0:T(8,128)S(1)} custom-call(f32[128,128]{1,0:T(8,128)S(1)} %convolution_subtract_fusion.4), custom_call_target="Cholesky" | custom-call | tf_op jit(solution)/shard_map/jit(cholesky)/cholesky | solution.py:14
  725.6 4.1 while.5
  726.2 1.4 bitcast_dynamic-update-slice_fusion.8
  728.3 1.4 bitcast_dynamic-update-slice_fusion.8
  730.4 20.5 %custom-call.31 = f32[2,128,128]{1,2,0:T(8,128)S(1)} custom-call(f32[2,128,128]{2,1,0:T(8,128)} %copy-done.12), custom_call_target="InvertDiagBlocksLowerTriangular" | custom-call | tf_op jit(solution)/shard_map/jit(_cho_solve)/triangular_solve | solution.py:15
  750.8 1.4 add_bitcast_fusion
  (118 shorter events, 43.4 us)
Async XLA Ops:
  7.2 2.2 copy-start
  7.2 161.2 %all-reduce.7.cloned.1.call-start = ((), (), s32[]{:S(2)}) async-start(), calls=%async_computation | async-start | bytes 524288 | tf_op jit(solution)/shard_map/psum | solution.py:24
  9.3 2.9 copy-start.1
  9.3 229.9 %all-reduce.11.cloned.1.call-start = ((), (), s32[]{:S(2)}) async-start(), calls=%async_computation.2 | async-start | bytes 2621440 | tf_op jit(solution)/shard_map/psum | solution.py:22
  12.2 1.1 copy-start.3
  12.2 1.9 copy-start.11
  13.3 669.3 %all-reduce.9.cloned.1.call-start = ((), (), s32[]{:S(2)}) async-start(), calls=%async_computation.1 | async-start | bytes 2621440 | tf_op jit(solution)/shard_map/psum | solution.py:31
  240.2 66.3 %copy-start.2 = (f32[4,256,256]{2,1,0:T(8,128)S(1)}, f32[4,256,256]{2,1,0:T(8,128)}, u32[]{:S(2)}) copy-start(f32[4,256,256]{2,1,0:T(8,128)} %get-tuple-element.61) | copy-start | bytes 3145732
  242.1 0.7 copy-start.7
  278.3 1.9 copy-start.6
  285.4 0.7 copy-start.13
  453.1 74.9 %copy-start.15 = (f32[4,256]{1,0:T(4,128)}, f32[4,256]{1,0:T(4,128)S(1)}, u32[]{:S(2)}) copy-start(f32[4,256]{1,0:T(4,128)S(1)} %fusion.36) | copy-start | bytes 12292
  457.1 0.7 copy-start.8
  493.3 2.6 copy-start.4
  501.1 0.7 copy-start.14
  522.4 1.8 copy-start.10
  685.5 0.7 copy-start.9
  722.0 2.6 copy-start.5
  729.7 0.7 copy-start.12
Sparse Core Ops, SparseCore 0:
  11.8 156.5 all-reduce.6
  171.0 68.1 all-reduce.10
  530.0 152.6 all-reduce.8
where the time goes:
time: 773 us; the launch traced here: 764 us
  waiting for transfers between devices  375 us (49%)
  other arithmetic  177 us (23%)
  blocking collectives  144 us (19%)
  matrix products  25.7 us (3%)
  local copies, waits for them, and re-layouts  23 us (3%)
  between operations  18.4 us (2%)
    psum x1, waiting for transfers between devices, body(): row_gram, frame_rhs = lax.psum((row_part, rhs_part), 'row')  153 us
    psum x1, waiting for transfers between devices, body(): lax.psum((jnp.sum(frame_factor[:, None, :] * products, axis=0), new_gram_...  150 us
    psum x1, blocking collectives, body(): row_gram, frame_rhs = lax.psum((row_part, rhs_part), 'row')  144 us
    another operation x20, other arithmetic, gram_solve(): lower_factor = jnp.linalg.cholesky(gram)  103 us
    psum x1, waiting for transfers between devices, body(): slab_products, col_gram = lax.psum((local_slab, col_part), 'col')  70.8 us
    another operation x7, other arithmetic, gram_solve(): return jax.scipy.linalg.cho_solve((lower_factor, True), rhs.T).T  64.6 us
  transfers between devices with their start and end apart: 3, of which 3 were waited for; matrix products, arithmetic and copies ran while one was open for 1% of the time, Pallas kernels for 0%

commit v1 on v0

v1 whole, which is shorter than its diff:
```python
import jax
import jax.numpy as jnp
from jax import lax
from jax.experimental import pallas as pl
from jax.experimental.pallas import tpu as pltpu
from jax.sharding import PartitionSpec as P

R = 256
HALF = 128
HIGHEST = lax.Precision.HIGHEST
F32 = jnp.float32


def inner_gram(matrix):
    return lax.dot_general(
        matrix, matrix, (((0,), (0,)), ((), ())), preferred_element_type=F32
    )


def matmul_f32(a, b, dims=((1,), (0,))):
    return lax.dot_general(a, b, (dims, ((), ())), precision=HIGHEST, preferred_element_type=F32)


def eliminate8(tile, g):
    lane = lax.broadcasted_iota(jnp.int32, (8, R), 1)
    cols = [jnp.broadcast_to(tile[:, g + j : g + j + 1], (8, HALF)) for j in range(8)]
    s = {}
    for j in range(8):
        for i in range(j, 8):
            s[i, j] = s[j, i] = jnp.broadcast_to(cols[j][i : i + 1, :], (8, HALF))
    inside = (lane >= g) & (lane < g + 8)
    rows = []
    for i in range(8):
        row = jnp.broadcast_to(tile[i : i + 1, :], (8, R))
        rows.append(jnp.where(inside, jnp.where(lane == g + i, 1.0, 0.0), row))
    for k in range(8):
        inv = 1.0 / s[k, k]
        p = {j: s[k, j] * inv for j in range(k + 1, 8)}
        rows[k] = rows[k] * jnp.concatenate([inv, inv], 1)
        new = {}
        for j in range(k + 1, 8):
            for i in range(8):
                if i == k or k < i < j:
                    continue
                new[i, j] = s[i, j] - s[i, k] * p[j]
        for i in range(8):
            if i != k:
                rows[i] = rows[i] - jnp.concatenate([s[i, k]] * 2, 1) * rows[k]
        for (i, j), v in new.items():
            s[i, j] = v
            if i > k:
                s[j, i] = v
        for j in range(k + 1, 8):
            s[k, j] = p[j]
    return rows


def spd_inverse(a):
    lane8 = lax.broadcasted_iota(jnp.int32, (8, R), 1)
    sub8 = lax.broadcasted_iota(jnp.int32, (8, R), 0)
    groups = HALF // 8
    for start in (0, HALF):
        tiles = [a[start + 8 * m : start + 8 * m + 8, :] for m in range(groups)]
        for b in range(groups):
            g = start + 8 * b
            rows = eliminate8(tiles[b], g)
            inside = (lane8 >= g) & (lane8 < g + 8)
            for m in list(range(b + 1, groups)) + list(range(b)):
                acc = [
                    jnp.broadcast_to(tiles[m][:, g + j : g + j + 1], (8, R)) * rows[j]
                    for j in range(8)
                ]
                while len(acc) > 1:
                    acc = [acc[i] + acc[i + 1] for i in range(0, len(acc), 2)]
                tiles[m] = jnp.where(inside, 0.0, tiles[m]) - acc[0]
            merged = rows[0]
            for j in range(1, 8):
                merged = jnp.where(sub8 == j, rows[j], merged)
            tiles[b] = merged
        panel = jnp.concatenate(tiles, 0)
        other = HALF - start
        rest = a[other : other + HALF, :]
        update = matmul_f32(rest[:, start : start + HALF], panel)
        lane = lax.broadcasted_iota(jnp.int32, (HALF, R), 1)
        inside = (lane >= start) & (lane < start + HALF)
        rest = jnp.where(inside, 0.0, rest) - update
        a = jnp.concatenate([panel, rest] if start == 0 else [rest, panel], 0)
    return a


def time_kernel(row_gram, col_gram, rhs, time_gram, factor_out, time_out, inverse_out):
    factor = matmul_f32(rhs[...], spd_inverse(row_gram[...] * col_gram[...]))
    factor_out[...] = factor
    time_new = time_gram[...] + matmul_f32(factor, factor, ((0,), (0,)))
    time_out[...] = time_new
    inverse_out[...] = spd_inverse(time_new * col_gram[...])


def col_kernel(time_new, gram, sums, out):
    inverse = spd_inverse(time_new[...] * gram[...])
    out[...] = matmul_f32(sums[...], inverse).astype(out.dtype)


def gather(x, axis, count):
    return lax.all_to_all(jnp.broadcast_to(x[None], (count,) + x.shape), axis, 0, 0)


def body(frames, row_factor, col_factor, row_history, col_history, time_gram):
    nrow = lax.axis_size("row")
    ncol = lax.axis_size("col")
    r = lax.axis_index("row")
    own = R // nrow
    row_part = inner_gram(row_factor)
    col_part = inner_gram(col_factor)
    slab_part = jnp.einsum("bij,jr->bir", frames, col_factor, preferred_element_type=F32)
    rhs_part = jnp.sum(slab_part * row_factor.astype(F32)[None], axis=1)
    slab_own = lax.psum_scatter(slab_part, "col", scatter_dimension=1, tiled=True)
    slab = lax.all_gather(slab_own, "col", axis=1, tiled=True)

    col_piece = lax.dynamic_slice_in_dim(col_part, own * r, own, 0)
    first = gather(jnp.concatenate([col_piece, rhs_part], 0), "col", ncol).sum(0)
    col_piece, rhs_part = first[:own], first[own:]

    nb = rhs_part.shape[0]
    rhs_pad = jnp.pad(
        rhs_part.reshape(nb, nrow, own).transpose(1, 0, 2), ((0, 0), (0, 0), (0, HALF - own))
    )
    second = jnp.concatenate([row_part.reshape(nrow, own, R), rhs_pad], 2)
    second = lax.all_to_all(second, "row", 0, 0).sum(0)
    third = gather(jnp.concatenate([second, col_piece], 1), "row", nrow)
    row_gram = third[:, :, :R].reshape(R, R)
    col_gram = third[:, :, R + HALF :].reshape(R, R)
    rhs = third[:, :, R : R + own].transpose(1, 0, 2).reshape(nb, R)

    square = jax.ShapeDtypeStruct((R, R), F32)
    frame_factor, time_new, inverse = pl.pallas_call(
        time_kernel,
        out_shape=(jax.ShapeDtypeStruct((nb, R), F32), square, square),
        name="time_solve",
    )(row_gram, col_gram, rhs, time_gram)

    row_sums = row_history + jnp.sum(frame_factor[:, None, :] * slab, axis=0)
    new_row = matmul_f32(row_sums, inverse).astype(jnp.bfloat16)
    gram_part = inner_gram(new_row)
    products = jnp.einsum("bij,ir->bjr", frames, new_row, preferred_element_type=F32)
    col_part = jnp.sum(frame_factor[:, None, :] * products, axis=0)
    high = gram_part.astype(jnp.bfloat16)
    low = (gram_part - high.astype(F32)).astype(jnp.bfloat16)
    chunk = col_part.shape[0] // nrow
    message = jnp.concatenate(
        [
            col_part.astype(jnp.bfloat16).reshape(nrow, chunk, R),
            high.reshape(nrow, own, R),
            low.reshape(nrow, own, R),
        ],
        1,
    )
    total = lax.all_to_all(message, "row", 0, 0).astype(F32).sum(0)
    gram_own = total[chunk : chunk + own] + total[chunk + own :]
    new_gram = gather(gram_own, "row", nrow).reshape(R, R)
    col_sums = lax.dynamic_slice_in_dim(col_history, chunk * r, chunk, 0) + total[:chunk]
    new_col_own = pl.pallas_call(
        col_kernel,
        out_shape=jax.ShapeDtypeStruct((chunk, R), jnp.bfloat16),
        name="col_solve",
    )(time_new, new_gram, col_sums)
    new_col = gather(new_col_own, "row", nrow).reshape(nrow * chunk, R)
    return (frame_factor, new_row, new_col)


def solution(mesh):
    in_specs = (
        P(None, "row", "col"),
        P("row", None),
        P("col", None),
        P("row", None),
        P("col", None),
        P(),
    )
    out_specs = (P(), P("row", None), P("col", None))
    return jax.shard_map(body, mesh=mesh, in_specs=in_specs, out_specs=out_specs, check_vma=False)
```

time: 773 us -> 210 us (0.27); the launches traced: 764 us -> 210 us
  waiting for transfers between devices: 375 us -> 15.6 us
  other arithmetic: 177 us -> 4.27 us
  Pallas kernels: 0 us -> 33.8 us
  blocking collectives: 144 us -> 113 us
  matrix products: 25.7 us -> 5.69 us
  local copies, waits for them, and re-layouts: 23 us -> 7.31 us
  starting transfers between devices: 0.12 us -> 15.8 us
    psum x3 -> x0, waiting for transfers between devices: 375 us -> none  [the longest x1 153 us: body(): row_gram, frame_rhs = lax.psum((row_part, rhs_part), 'row')]
    another operation x27 -> x0, other arithmetic: 168 us -> none  [the longest x20 103 us: gram_solve(): lower_factor = jnp.linalg.cholesky(gram)]
    psum x1 -> x0, blocking collectives: 144 us -> none  [body(): row_gram, frame_rhs = lax.psum((row_part, rhs_part), 'row')]
    all_to_all x0 -> x4, blocking collectives: none -> 113 us  [the longest x2 52.6 us: gather(): lax.all_to_all(jnp.broadcast_to(x[None], (count,) + x.shape), axis, 0, 0)]
    pallas_call x0 -> x2, Pallas kernels: none -> 33.8 us  [the longest x1 22.1 us: body(): pl.pallas_call(time_kernel, out_shape=(jax.ShapeDtypeStruct((nb, R), F32)...]
    all_to_all x0 -> x2, starting transfers between devices: none -> 15.7 us  [gather(): lax.all_to_all(jnp.broadcast_to(x[None], (count,) + x.shape), axis, 0, 0)]
    all_to_all x0 -> x2, waiting for transfers between devices: none -> 15.5 us  [gather(): lax.all_to_all(jnp.broadcast_to(x[None], (count,) + x.shape), axis, 0, 0)]
    another operation x24 -> x0, matrix products: 14.9 us -> none  [the longest x18 8.45 us: gram_solve(): return jax.scipy.linalg.cho_solve((lower_factor, True), rhs.T).T]
  transfers between devices with their start and end apart: 3 -> 4, of which waited for: 3 -> 2; matrix products, arithmetic and copies ran while one was open for 1% -> 3% of each run, Pallas kernels for 0% -> 11%
where the time goes in v1:
time: 210 us
  blocking collectives  113 us (54%)
  Pallas kernels  33.8 us (16%)
  starting transfers between devices  15.8 us (8%)
  waiting for transfers between devices  15.6 us (7%)
  between operations  14.3 us (7%)
  local copies, waits for them, and re-layouts  7.31 us (3%)
  matrix products  5.69 us (3%)
  other arithmetic  4.27 us (2%)
    all_to_all x2, blocking collectives, gather(): lax.all_to_all(jnp.broadcast_to(x[None], (count,) + x.shape), axis, 0, 0)  52.6 us
    all_to_all x1, blocking collectives, body(): total = lax.all_to_all(message, 'row', 0, 0).astype(F32).sum(0)  31.1 us
    all_to_all x1, blocking collectives, body(): second = lax.all_to_all(second, 'row', 0, 0).sum(0)  29.3 us
    pallas_call x1, Pallas kernels, body(): pl.pallas_call(time_kernel, out_shape=(jax.ShapeDtypeStruct((nb, R), F32)...  22.1 us
    all_to_all x2, starting transfers between devices, gather(): lax.all_to_all(jnp.broadcast_to(x[None], (count,) + x.shape), axis, 0, 0)  15.7 us
    all_to_all x2, waiting for transfers between devices, gather(): lax.all_to_all(jnp.broadcast_to(x[None], (count,) + x.shape), axis, 0, 0)  15.5 us
    pallas_call x1, Pallas kernels, body(): pl.pallas_call(col_kernel, out_shape=jax.ShapeDtypeStruct((chunk, R), jnp...  11.7 us
  transfers between devices with their start and end apart: 4, of which 2 were waited for; matrix products, arithmetic and copies ran while one was open for 3% of the time, Pallas kernels for 11%

profile of v1, /device:TPU:6, one launch (start us, length us, event | category | flops | bytes accessed | tf_op | source)
XLA Modules:
  0.0 209.7 jit_solution(12292094328325668675)
XLA Ops:
  7.2 1.1 convert_element_type.27
  8.3 0.5 copy-done
  8.8 2.8 %multiply_reduce_fusion.1 = (f32[4,256]{1,0:T(4,128)S(1)}, f32[4,256,256]{2,1,0:T(8,128)}) fusion(f32[256,256]{1,0:T(8,128)S(1)} %convert_element_type.27, bf16[4,256,1024]{2,1,0:T(8,128)(2,1)S(1)} %copy-done, bf16[1024,256]{1,0:T(8,128)(2,1)} %param.8), kind=kOutput, calls=%fused_computation.5 | convolution fusion | flops 537394176 | bytes 3936256 | tf_op jit(solution)/shard_map/bij,jr->bir/dot_general | solution.py:115
  11.7 0.3 fusion.8
  12.1 0.6 broadcast_in_dim.8
  12.7 9.1 %all-to-all-start = ((f32[8,8,256]{2,1,0:T(8,128)}), f32[8,8,256]{2,1,0:T(8,128)S(1)}, u32[]{:S(2)}, u32[]{:S(2)}) async-start(f32[8,8,256]{2,1,0:T(8,128)} %broadcast_in_dim.8), calls=%async_computation | async-start | bytes 131072 | tf_op jit(solution)/shard_map/all_to_all | solution.py:105
  21.8 0.2 fusion.7
  22.2 3.2 %all-to-all-done = f32[8,8,256]{2,1,0:T(8,128)S(1)} async-done(((f32[8,8,256]{2,1,0:T(8,128)}), f32[8,8,256]{2,1,0:T(8,128)S(1)}, u32[]{:S(2)}, u32[]{:S(2)}) %all-to-all-start) | async-done | bytes 65568 | tf_op jit(solution)/shard_map/all_to_all | solution.py:105
  25.4 0.1 reshape.43
  25.7 29.3 %all_to_all.30 = f32[64,4,384]{2,1,0:T(4,128)S(1)} all-to-all(f32[64,4,384]{2,1,0:T(4,128)S(1)} %select_maximum_fusion), channel_id=1, replica_groups=mesh['row'=64,'col'=8] {'row'}, dimensions={0} | all-to-all | bytes 786432 | tf_op jit(solution)/shard_map/all_to_all | solution.py:129
  55.2 31.3 %all_to_all.31 = f32[64,4,640]{2,1,0:T(4,128)S(1)} all-to-all(f32[64,4,640]{2,1,0:T(4,128)S(1)} %broadcast_in_dim.9), channel_id=1, replica_groups=mesh['row'=64,'col'=8] {'row'}, dimensions={0} | all-to-all | bytes 1310720 | tf_op jit(solution)/shard_map/all_to_all | solution.py:105
  86.5 0.8 reshape.45.col_gram
  87.4 0.7 reshape.46.rhs
  88.1 0.8 reshape.44.row_gram
  88.9 22.1 %time_solve.1 = (f32[4,256]{1,0:T(4,128)}, f32[256,256]{1,0:T(8,128)}, f32[256,256]{1,0:T(8,128)}) custom-call(f32[256,256]{1,0:T(8,128)} %reshape.44.row_gram, f32[256,256]{1,0:T(8,128)} %reshape.45.col_gram, f32[4,256]{1,0:T(4,128)} %reshape.46.rhs, f32[256,256]{1,0:T(8,128)} %time_gram.1), custom_call_target="tpu_custom_call" | custom-call | tf_op jit(solution)/shard_map/time_solve/pallas_call | solution.py:136
  111.0 1.3 multiply_reduce_fusion
  112.3 1.3 convolution_convert_fusion
  113.7 0.2 subtract_convert_fusion
  113.9 0.8 fusion
  114.8 0.2 copy.28
  115.0 0.2 pad_maximum_fusion
  115.2 31.1 %all_to_all.32 = bf16[64,24,256]{2,1,0:T(8,128)(2,1)S(1)} all-to-all(bf16[64,24,256]{2,1,0:T(8,128)(2,1)S(1)} %pad_maximum_fusion), channel_id=1, replica_groups=mesh['row'=64,'col'=8] {'row'}, dimensions={0} | all-to-all | bytes 1572864 | tf_op jit(solution)/shard_map/all_to_all | solution.py:158
  146.3 0.1 convert_reduce_fusion
  146.4 0.7 broadcast_in_dim.10
  147.2 6.6 %all-to-all-start.4 = ((f32[64,4,256]{2,1,0:T(4,128)}), f32[64,4,256]{2,1,0:T(4,128)S(1)}, u32[]{:S(2)}, u32[]{:S(2)}) async-start(f32[64,4,256]{2,1,0:T(4,128)} %broadcast_in_dim.10), calls=%async_computation.5 | async-start | bytes 524288 | tf_op jit(solution)/shard_map/all_to_all | solution.py:105
  153.8 1.3 slice_add_fusion.sums
  155.1 12.3 %all-to-all-done.4 = f32[64,4,256]{2,1,0:T(4,128)S(1)} async-done(((f32[64,4,256]{2,1,0:T(4,128)}), f32[64,4,256]{2,1,0:T(4,128)S(1)}, u32[]{:S(2)}, u32[]{:S(2)}) %all-to-all-start.4) | async-done | bytes 262176 | tf_op jit(solution)/shard_map/all_to_all | solution.py:105
  167.4 0.8 reshape.49.gram
  168.2 11.7 %col_solve.1 = bf16[16,256]{1,0:T(8,128)(2,1)} custom-call(f32[256,256]{1,0:T(8,128)} %get-tuple-element.8.time_new, f32[256,256]{1,0:T(8,128)} %reshape.49.gram, f32[16,256]{1,0:T(8,128)} %slice_add_fusion.sums), custom_call_target="tpu_custom_call" | custom-call | tf_op jit(solution)/shard_map/col_solve/pallas_call | solution.py:162
  180.0 0.7 broadcast_in_dim.11
  180.7 21.3 %all_to_all.33 = bf16[64,16,256]{2,1,0:T(8,128)(2,1)S(1)} all-to-all(bf16[64,16,256]{2,1,0:T(8,128)(2,1)S(1)} %broadcast_in_dim.11), channel_id=1, replica_groups=mesh['row'=64,'col'=8] {'row'}, dimensions={0} | all-to-all | bytes 1048576 | tf_op jit(solution)/shard_map/all_to_all | solution.py:105
  202.0 0.8 copy.33
  (33 shorter events, 0.7 us)
Async XLA Ops:
  7.2 1.7 copy-start
  7.2 47.9 %reduce-scatter.2.cloned.1.call-start = ((), (), s32[]{:S(2)}) async-start(), calls=%async_computation.7 | async-start | bytes 1179648 | tf_op jit(solution)/shard_map/reduce_scatter | solution.py:117
  8.8 2.9 %copy-start.1 = (bf16[1024,256]{1,0:T(8,128)(2,1)S(1)}, bf16[1024,256]{1,0:T(8,128)(2,1)}, u32[]{:S(2)}) copy-start(bf16[1024,256]{1,0:T(8,128)(2,1)} %param.8) | copy-start | bytes 1572868
  11.6 10.2 %copy-start.2 = (bf16[256,256]{1,0:T(8,128)(2,1)S(1)}, bf16[256,256]{1,0:T(8,128)(2,1)}, u32[]{:S(2)}) copy-start(bf16[256,256]{1,0:T(8,128)(2,1)} %param.7) | copy-start | bytes 393220
  12.7 12.7 %all-to-all-start = ((f32[8,8,256]{2,1,0:T(8,128)}), f32[8,8,256]{2,1,0:T(8,128)S(1)}, u32[]{:S(2)}, u32[]{:S(2)}) async-start(f32[8,8,256]{2,1,0:T(8,128)} %broadcast_in_dim.8), calls=%async_computation | async-start | bytes 131072 | tf_op jit(solution)/shard_map/all_to_all | solution.py:105
  21.8 89.1 %all-gather.2.cloned.1.call-start = ((), (), s32[]{:S(2)}) async-start(), calls=%async_computation.8 | async-start | bytes 1179648 | tf_op jit(solution)/shard_map/all_gather | solution.py:118
  86.5 25.8 %copy-start.4 = (f32[256,256]{1,0:T(8,128)S(1)}, f32[256,256]{1,0:T(8,128)}, u32[]{:S(2)}) copy-start(f32[256,256]{1,0:T(8,128)} %param.9) | copy-start | bytes 786436
  111.0 2.9 %copy-start.5 = (f32[4,256]{1,0:T(4,128)S(1)}, f32[4,256]{1,0:T(4,128)}, u32[]{:S(2)}) copy-start(f32[4,256]{1,0:T(4,128)} %get-tuple-element.20) | copy-start | bytes 12292
  113.7 1.0 copy-start.3
  147.2 20.3 %all-to-all-start.4 = ((f32[64,4,256]{2,1,0:T(4,128)}), f32[64,4,256]{2,1,0:T(4,128)S(1)}, u32[]{:S(2)}, u32[]{:S(2)}) async-start(f32[64,4,256]{2,1,0:T(4,128)} %broadcast_in_dim.10), calls=%async_computation.5 | async-start | bytes 524288 | tf_op jit(solution)/shard_map/all_to_all | solution.py:105
Sparse Core Ops, SparseCore 0:
  11.8 39.0 reduce-scatter.1
  55.3 27.1 all-gather.1

commit v2 on v1

v2 whole, which is shorter than its diff:
```python
import jax
import jax.numpy as jnp
from jax import lax
from jax.experimental import pallas as pl
from jax.experimental.pallas import tpu as pltpu
from jax.sharding import PartitionSpec as P

R = 256
HALF = 128
HIGHEST = lax.Precision.HIGHEST
F32 = jnp.float32


def inner_gram(matrix):
    return lax.dot_general(
        matrix, matrix, (((0,), (0,)), ((), ())), preferred_element_type=F32
    )


def matmul_f32(a, b, dims=((1,), (0,))):
    return lax.dot_general(a, b, (dims, ((), ())), precision=HIGHEST, preferred_element_type=F32)


def eliminate8(tile, g):
    lane = lax.broadcasted_iota(jnp.int32, (8, R), 1)
    cols = [jnp.broadcast_to(tile[:, g + j : g + j + 1], (8, HALF)) for j in range(8)]
    s = {}
    for j in range(8):
        for i in range(j, 8):
            s[i, j] = s[j, i] = jnp.broadcast_to(cols[j][i : i + 1, :], (8, HALF))
    inside = (lane >= g) & (lane < g + 8)
    rows = []
    for i in range(8):
        row = jnp.broadcast_to(tile[i : i + 1, :], (8, R))
        rows.append(jnp.where(inside, jnp.where(lane == g + i, 1.0, 0.0), row))
    for k in range(8):
        inv = pl.reciprocal(s[k, k])
        p = {j: s[k, j] * inv for j in range(k + 1, 8)}
        rows[k] = rows[k] * jnp.concatenate([inv, inv], 1)
        new = {}
        for j in range(k + 1, 8):
            for i in range(8):
                if i == k or k < i < j:
                    continue
                new[i, j] = s[i, j] - s[i, k] * p[j]
        for i in range(8):
            if i != k:
                rows[i] = rows[i] - jnp.concatenate([s[i, k]] * 2, 1) * rows[k]
        for (i, j), v in new.items():
            s[i, j] = v
            if i > k:
                s[j, i] = v
        for j in range(k + 1, 8):
            s[k, j] = p[j]
    return rows


def half_inverse(m):
    lane8 = lax.broadcasted_iota(jnp.int32, (8, R), 1)
    sub8 = lax.broadcasted_iota(jnp.int32, (8, R), 0)
    groups = HALF // 8
    tiles = [m[8 * i : 8 * i + 8, :] for i in range(groups)]
    for b in range(groups):
        g = 8 * b
        rows = eliminate8(tiles[b], g)
        inside = (lane8 >= g) & (lane8 < g + 8)
        for i in list(range(b + 1, groups)) + list(range(b)):
            acc = [
                jnp.broadcast_to(tiles[i][:, g + j : g + j + 1], (8, R)) * rows[j]
                for j in range(8)
            ]
            while len(acc) > 1:
                acc = [acc[k] + acc[k + 1] for k in range(0, len(acc), 2)]
            tiles[i] = jnp.where(inside, 0.0, tiles[i]) - acc[0]
        merged = rows[0]
        for j in range(1, 8):
            merged = jnp.where(sub8 == j, rows[j], merged)
        tiles[b] = merged
    panel = jnp.concatenate(tiles, 0)
    rest = m[HALF:, :]
    update = matmul_f32(rest[:, :HALF], panel)
    m[:HALF, :HALF] = rest[:, HALF:] - update[:, HALF:]
    m[:HALF, HALF:] = -update[:, :HALF]
    m[HALF:, :HALF] = panel[:, HALF:]
    m[HALF:, HALF:] = panel[:, :HALF]


def square_iota():
    return (
        lax.broadcasted_iota(jnp.int32, (HALF, HALF), 0),
        lax.broadcasted_iota(jnp.int32, (HALF, HALF), 1),
    )


def pack_gram(gram, tiles):
    i, j = square_iota()
    low = gram[HALF:, HALF:]
    packed = (gram[:HALF, HALF:], jnp.where(i >= j, gram[:HALF, :HALF], low))
    diag = jnp.sum(jnp.where(i == j, low, 0.0), 0, keepdims=True)
    sub = lax.broadcasted_iota(jnp.int32, (8, HALF), 0)
    tail = jnp.where(sub == 4, diag, 0.0)
    for q in range(32):
        rows = packed[q // 16][8 * (q % 16) : 8 * (q % 16) + 8]
        tiles[2 * q] = jnp.where(sub < 4, rows, tail)
        tiles[2 * q + 1] = jnp.where(sub < 4, pltpu.roll(rows, 4, 0), tail)


def unpack_gram(rows, diag):
    i, j = square_iota()
    upper = jnp.concatenate(rows[:16], 0)
    both = jnp.concatenate(rows[16:], 0)
    flip = both.T
    first = jnp.where(i >= j, both, flip)
    second = jnp.where(i < j, both, jnp.where(i == j, diag, flip))
    return jnp.concatenate(
        [jnp.concatenate([first, upper], 1), jnp.concatenate([upper.T, second], 1)], 0
    )


def local_kernel(index, frames, row_factor, col_factor, slab_out, message, tiles):
    rows = row_factor[...].astype(F32)
    sums = []
    for b in range(frames.shape[0]):
        slab = jnp.dot(frames[b], col_factor[...], preferred_element_type=F32)
        slab_out[b] = slab
        sums.append(jnp.sum(slab * rows, 0, keepdims=True))
    pack_gram(inner_gram(col_factor[...]), tiles)
    own = tiles[index[0]]
    sums = jnp.concatenate([x[:, :HALF] for x in sums] + [x[:, HALF:] for x in sums], 0)
    for i in range(message.shape[0]):
        message[i, :8] = own
        message[i, 8:] = sums


def row_pack_kernel(factor, out):
    pack_gram(inner_gram(factor[...]), out)


def time_kernel(
    parts, row_parts, diags, time_gram, factor_out, time_out, inverse_out, col_gram
):
    sub = lax.broadcasted_iota(jnp.int32, (8, HALF), 0)
    row_rows, col_rows = [], []
    for q in range(32):
        even, odd = parts[2 * q], parts[2 * q + 1]
        row_rows.append(jnp.where(sub < 4, even, pltpu.roll(odd, 4, 0)))
        even = jnp.where(sub < 7, even, pltpu.roll(row_parts[2 * q], 2, 0))
        odd = jnp.where(sub < 7, odd, pltpu.roll(row_parts[2 * q + 1], 2, 0))
        col_rows.append(jnp.where(sub < 4, pltpu.roll(even, 4, 0), odd))
    col = unpack_gram(col_rows, diags[1:2, :])
    col_gram[...] = col
    inverse_out[...] = unpack_gram(row_rows, diags[0:1, :]) * col
    each = parts.shape[0] // 8
    rhs = [parts[each * i][7:8, :] for i in range(8)]
    rhs = jnp.concatenate(
        [jnp.concatenate(rhs[:4], 0), jnp.concatenate(rhs[4:], 0)], 1
    )

    @pl.loop(0, 4)
    def _(step):
        half_inverse(inverse_out)

        @pl.when(step == 1)
        def _():
            factor = matmul_f32(rhs, inverse_out[...])
            factor_out[...] = factor
            time_new = time_gram[...] + matmul_f32(factor, factor, ((0,), (0,)))
            time_out[...] = time_new
            inverse_out[...] = time_new * col_gram[...]


def split_gram(gram):
    high = gram.astype(jnp.bfloat16)
    return high, (gram - high.astype(F32)).astype(jnp.bfloat16)


def col_kernel(time_new, history, parts, out, inverse, sums):
    sub = lax.broadcasted_iota(jnp.int32, (8, R), 0)
    chunk = history.shape[0] // parts.shape[0]
    for q in range(32):
        rows = []
        for p in (2 * q, 2 * q + 1):
            part = parts[p].astype(F32)
            sums[chunk * p : chunk * p + chunk, :] = (
                history[chunk * p : chunk * p + chunk, :] + part[:chunk]
            )
            part = part[chunk:]
            rows.append(part + pltpu.roll(part, 4, 0))
        gram = jnp.where(sub < 4, rows[0], rows[1])
        inverse[8 * q : 8 * q + 8, :] = time_new[8 * q : 8 * q + 8, :] * gram

    @pl.loop(0, 2)
    def _(step):
        half_inverse(inverse)

    out[...] = matmul_f32(sums[...], inverse[...]).astype(out.dtype)


def gather(x, axis, count):
    return lax.all_to_all(jnp.broadcast_to(x[None], (count,) + x.shape), axis, 0, 0)


def body(frames, row_factor, col_factor, row_history, col_history, time_gram):
    nrow = lax.axis_size("row")
    ncol = lax.axis_size("col")
    nb = frames.shape[0]
    r = lax.axis_index("row")
    own = R // nrow
    square = jax.ShapeDtypeStruct((R, R), F32)
    tiles = jax.ShapeDtypeStruct((nrow, 8, HALF), F32)
    vmem = pl.BlockSpec(memory_space=pltpu.VMEM)
    slab_part, col_parts = pl.pallas_call(
        local_kernel,
        out_shape=(
            jax.ShapeDtypeStruct((nb,) + row_history.shape, F32),
            jax.ShapeDtypeStruct((ncol, 16, HALF), F32),
        ),
        in_specs=[pl.BlockSpec(memory_space=pltpu.SMEM), vmem, vmem, vmem],
        scratch_shapes=[pltpu.VMEM(tiles.shape, F32)],
        name="local_products",
    )(r.reshape(1), frames, row_factor, col_factor)
    slab_own = lax.psum_scatter(slab_part, "col", scatter_dimension=1, tiled=True)
    col_parts = lax.all_to_all(col_parts, "col", 0, 0).sum(0)
    row_tiles = pl.pallas_call(row_pack_kernel, out_shape=tiles, name="row_pack")(row_factor)
    sub = lax.broadcasted_iota(jnp.int32, tiles.shape, 1)
    rhs_rows = jnp.repeat(col_parts[8:], nrow // 8, axis=0)[:, None, :]
    row_tiles = jnp.where(
        sub < 5, row_tiles, jnp.where(sub == 5, col_parts[3][None, None], rhs_rows)
    )
    row_parts = lax.all_to_all(row_tiles, "row", 0, 0)
    row_own = row_parts.sum(0)
    message = jnp.concatenate([row_own[:4], col_parts[:3], row_own[6:7]], 0)
    diags = jnp.concatenate([row_own[4:5], col_parts[4:5], row_own[2:8]], 0)
    slab_own, message, diags = lax.optimization_barrier((slab_own, message, diags))
    parts = gather(message, "row", nrow)
    slab = lax.all_gather(slab_own, "col", axis=1, tiled=True)
    frame_factor, time_new, inverse = pl.pallas_call(
        time_kernel,
        out_shape=(jax.ShapeDtypeStruct((nb, R), F32), square, square),
        scratch_shapes=[pltpu.VMEM((R, R), F32)],
        name="time_solve",
    )(parts, row_parts, diags, time_gram)

    row_sums = row_history + jnp.sum(frame_factor[:, None, :] * slab, axis=0)
    new_row = matmul_f32(row_sums, inverse).astype(jnp.bfloat16)
    high, low = split_gram(inner_gram(new_row))
    products = jnp.einsum("bij,ir->bjr", frames, new_row, preferred_element_type=F32)
    col_part = jnp.sum(frame_factor[:, None, :] * products, axis=0)
    chunk = col_part.shape[0] // nrow
    message = jnp.concatenate(
        [
            col_part.astype(jnp.bfloat16).reshape(nrow, chunk, R),
            high.reshape(nrow, own, R),
            low.reshape(nrow, own, R),
        ],
        1,
    )
    total = lax.all_to_all(message, "row", 0, 0).astype(F32).sum(0)
    high, low = split_gram(total[chunk : chunk + own] + total[chunk + own :])
    total = jnp.concatenate([total[:chunk].astype(jnp.bfloat16), high, low], 0)
    new_col = pl.pallas_call(
        col_kernel,
        out_shape=jax.ShapeDtypeStruct(col_history.shape, jnp.bfloat16),
        scratch_shapes=[pltpu.VMEM((R, R), F32), pltpu.VMEM(col_history.shape, F32)],
        name="col_solve",
    )(time_new, col_history, gather(total, "row", nrow))
    return (frame_factor, new_row, new_col)


def solution(mesh):
    in_specs = (
        P(None, "row", "col"),
        P("row", None),
        P("col", None),
        P("row", None),
        P("col", None),
        P(),
    )
    out_specs = (P(), P("row", None), P("col", None))
    return jax.shard_map(body, mesh=mesh, in_specs=in_specs, out_specs=out_specs, check_vma=False)
```

time: 210 us -> 185 us (0.88)
  blocking collectives: 113 us -> 84.5 us
  Pallas kernels: 33.8 us -> 41 us
  local copies, waits for them, and re-layouts: 7.31 us -> 0.41 us
  starting transfers between devices: 15.8 us -> 21.5 us
  matrix products: 5.69 us -> 2.32 us
    all_to_all x1 -> x0, blocking collectives: 29.3 us -> none  [body(): second = lax.all_to_all(second, 'row', 0, 0).sum(0)]
    pallas_call x1 -> x3, Pallas kernels: 11.7 us -> 18.6 us  [the longest x1 13.2 us: body(): pl.pallas_call(col_kernel, out_shape=jax.ShapeDtypeStruct(col_history.sha...]
    all_to_all x2, starting transfers between devices: 15.7 us -> 21.4 us  [the longest x1 12.2 us: body(): row_parts = lax.all_to_all(row_tiles, 'row', 0, 0)]
    all_to_all x2, blocking collectives: 52.6 us -> 56.1 us  [gather(): lax.all_to_all(jnp.broadcast_to(x[None], (count,) + x.shape), axis, 0, 0)]
    reshape x6 -> x0, local copies, waits for them, and re-layouts: 3.31 us -> none  [the longest x1 0.8 us: body(): col_gram = third[:, :, R + HALF:].reshape(R, R)]
    dot_general x1 -> x0, matrix products: 2.82 us -> none  [body(): jnp.einsum('bij,jr->bir', frames, col_factor, preferred_element_type=F32)]
    all_to_all x1, blocking collectives: 31.1 us -> 28.4 us  [body(): total = lax.all_to_all(message, 'row', 0, 0).astype(F32).sum(0)]
    broadcast_in_dim x4 -> x2, local copies, waits for them, and re-layouts: 2.19 us -> 0.07 us  [gather(): jnp.broadcast_to(x[None], (count,) + x.shape)]
  transfers between devices with their start and end apart: 4 -> 4, of which waited for: 2 -> 2; matrix products, arithmetic and copies ran while one was open for 3% -> 1% of each run, Pallas kernels for 11% -> 13%
where the time goes in v2:
time: 185 us
  blocking collectives  84.5 us (46%)
  Pallas kernels  41 us (22%)
  starting transfers between devices  21.5 us (12%)
  waiting for transfers between devices  16.5 us (9%)
  between operations  14.2 us (8%)
  other arithmetic  4.18 us (2%)
  matrix products  2.32 us (1%)
    all_to_all x2, blocking collectives, gather(): lax.all_to_all(jnp.broadcast_to(x[None], (count,) + x.shape), axis, 0, 0)  56.1 us
    all_to_all x1, blocking collectives, body(): total = lax.all_to_all(message, 'row', 0, 0).astype(F32).sum(0)  28.4 us
    pallas_call x1, Pallas kernels, body(): pl.pallas_call(time_kernel, out_shape=(jax.ShapeDtypeStruct((nb, R), F32)...  22.4 us
    all_to_all x1, waiting for transfers between devices, body(): row_parts = lax.all_to_all(row_tiles, 'row', 0, 0)  14.8 us
    pallas_call x1, Pallas kernels, body(): pl.pallas_call(col_kernel, out_shape=jax.ShapeDtypeStruct(col_history.sha...  13.2 us
    all_to_all x1, starting transfers between devices, body(): row_parts = lax.all_to_all(row_tiles, 'row', 0, 0)  12.2 us
    all_to_all x1, starting transfers between devices, body(): col_parts = lax.all_to_all(col_parts, 'col', 0, 0).sum(0)  9.15 us
  transfers between devices with their start and end apart: 4, of which 2 were waited for; matrix products, arithmetic and copies ran while one was open for 1% of the time, Pallas kernels for 13%

profile of v2, /device:TPU:6, one launch (start us, length us, event | category | flops | bytes accessed | tf_op | source)
XLA Modules:
  0.0 184.6 jit_solution(14590658707281372117)
XLA Ops:
  7.2 0.0 reduce-scatter.2.cloned.1.call-start
  7.2 3.6 %local_products.1 = (f32[4,256,256]{2,1,0:T(8,128)}, f32[8,16,128]{2,1,0:T(8,128)}) custom-call(s32[1]{0:T(128)} %bitcast.index, bf16[4,256,1024]{2,1,0:T(8,128)(2,1)} %frames.1, bf16[256,256]{1,0:T(8,128)(2,1)} %factor.1, bf16[1024,256]{1,0:T(8,128)(2,1)} %col_factor.1), custom_call_target="tpu_custom_call" | custom-call | tf_op jit(solution)/shard_map/local_products/pallas_call | solution.py:212
  10.8 0.0 reduce-scatter.2.cloned.1.call-update
  10.8 9.2 %all-to-all-start = ((f32[8,16,128]{2,1,0:T(8,128)}), f32[8,16,128]{2,1,0:T(8,128)S(1)}, u32[]{:S(2)}, u32[]{:S(2)}) async-start(f32[8,16,128]{2,1,0:T(8,128)} %get-tuple-element.12), calls=%async_computation.1 | async-start | bytes 131072 | tf_op jit(solution)/shard_map/all_to_all | solution.py:223
  20.0 1.8 row_pack.1
  21.8 1.7 all-to-all-done
  23.5 0.0 copy-start.3
  23.6 1.8 select_select_fusion
  25.3 12.2 %all-to-all-start.1 = ((f32[64,8,128]{2,1,0:T(8,128)}), f32[64,8,128]{2,1,0:T(8,128)S(1)}, u32[]{:S(2)}, u32[]{:S(2)}) async-start(f32[64,8,128]{2,1,0:T(8,128)} %select_select_fusion), calls=%async_computation.2 | async-start | bytes 524288 | tf_op jit(solution)/shard_map/all_to_all | solution.py:230
  37.6 0.0 all-gather.2.cloned.1.call-start
  37.7 14.8 %all-to-all-done.1.row_parts = f32[64,8,128]{2,1,0:T(8,128)S(1)} async-done(((f32[64,8,128]{2,1,0:T(8,128)}), f32[64,8,128]{2,1,0:T(8,128)S(1)}, u32[]{:S(2)}, u32[]{:S(2)}) %all-to-all-start.1) | async-done | bytes 262176 | tf_op jit(solution)/shard_map/all_to_all | solution.py:230
  52.4 0.1 reduce_sum.46
  52.5 0.6 pad_maximum_fusion.3.diags
  53.2 0.0 all-gather.2.cloned.1.call-update
  53.2 0.0 copy-start.1
  53.2 25.8 %all_to_all.25.parts = f32[64,8,128]{2,1,0:T(8,128)} all-to-all(f32[64,8,128]{2,1,0:T(8,128)S(1)} %broadcast_in_dim.42), channel_id=1, replica_groups=mesh['row'=64,'col'=8] {'row'}, dimensions={0} | all-to-all | bytes 524288 | tf_op jit(solution)/shard_map/all_to_all | solution.py:200
  79.0 0.0 copy-done
  79.0 22.4 %time_solve.1 = (f32[4,256]{1,0:T(4,128)}, f32[256,256]{1,0:T(8,128)}, f32[256,256]{1,0:T(8,128)}) custom-call(f32[64,8,128]{2,1,0:T(8,128)} %all_to_all.25.parts, f32[64,8,128]{2,1,0:T(8,128)} %copy-done, f32[8,128]{1,0:T(8,128)} %pad_maximum_fusion.3.diags, f32[256,256]{1,0:T(8,128)} %time_gram.1), custom_call_target="tpu_custom_call" | custom-call | tf_op jit(solution)/shard_map/time_solve/pallas_call | solution.py:237
  101.4 1.3 multiply_reduce_fusion
  102.7 0.0 copy-done.3
  102.8 1.3 convolution_convert_fusion
  104.1 0.0 copy-start.2
  104.1 0.2 subtract_convert_fusion
  104.3 0.0 copy-done.1
  104.4 0.8 fusion
  105.2 0.2 copy.14
  105.4 0.2 pad_maximum_fusion
  105.6 28.4 %all_to_all.26 = bf16[64,24,256]{2,1,0:T(8,128)(2,1)S(1)} all-to-all(bf16[64,24,256]{2,1,0:T(8,128)(2,1)S(1)} %pad_maximum_fusion), channel_id=1, replica_groups=mesh['row'=64,'col'=8] {'row'}, dimensions={0} | all-to-all | bytes 1572864 | tf_op jit(solution)/shard_map/all_to_all | solution.py:258
  134.0 0.1 convert_reduce_fusion
  134.2 0.1 broadcast_in_dim.43
  134.3 30.3 %all_to_all.27.parts = bf16[64,24,256]{2,1,0:T(8,128)(2,1)} all-to-all(bf16[64,24,256]{2,1,0:T(8,128)(2,1)S(1)} %broadcast_in_dim.43), channel_id=1, replica_groups=mesh['row'=64,'col'=8] {'row'}, dimensions={0} | all-to-all | bytes 1572864 | tf_op jit(solution)/shard_map/all_to_all | solution.py:200
  164.5 13.2 %col_solve.1 = bf16[1024,256]{1,0:T(8,128)(2,1)} custom-call(f32[256,256]{1,0:T(8,128)} %get-tuple-element.18.time_new, f32[1024,256]{1,0:T(8,128)} %history.1, bf16[64,24,256]{2,1,0:T(8,128)(2,1)} %all_to_all.27.parts), custom_call_target="tpu_custom_call" | custom-call | tf_op jit(solution)/shard_map/col_solve/pallas_call | solution.py:261
  (22 shorter events, 0.2 us)
Async XLA Ops:
  7.2 46.0 %reduce-scatter.2.cloned.1.call-start = ((), (), s32[]{:S(2)}) async-start(), calls=%async_computation.6 | async-start | bytes 1179648 | tf_op jit(solution)/shard_map/reduce_scatter | solution.py:222
  10.8 12.7 %all-to-all-start = ((f32[8,16,128]{2,1,0:T(8,128)}), f32[8,16,128]{2,1,0:T(8,128)S(1)}, u32[]{:S(2)}, u32[]{:S(2)}) async-start(f32[8,16,128]{2,1,0:T(8,128)} %get-tuple-element.12), calls=%async_computation.1 | async-start | bytes 131072 | tf_op jit(solution)/shard_map/all_to_all | solution.py:223
  23.5 79.2 %copy-start.3 = (f32[256,256]{1,0:T(8,128)S(1)}, f32[256,256]{1,0:T(8,128)}, u32[]{:S(2)}) copy-start(f32[256,256]{1,0:T(8,128)} %param.9) | copy-start | bytes 786436
  25.3 27.1 %all-to-all-start.1 = ((f32[64,8,128]{2,1,0:T(8,128)}), f32[64,8,128]{2,1,0:T(8,128)S(1)}, u32[]{:S(2)}, u32[]{:S(2)}) async-start(f32[64,8,128]{2,1,0:T(8,128)} %select_select_fusion), calls=%async_computation.2 | async-start | bytes 524288 | tf_op jit(solution)/shard_map/all_to_all | solution.py:230
  37.6 63.8 %all-gather.2.cloned.1.call-start = ((), (), s32[]{:S(2)}) async-start(), calls=%async_computation.7 | async-start | bytes 1179648 | tf_op jit(solution)/shard_map/all_gather | solution.py:236
  52.4 26.6 %copy-start = (f32[64,8,128]{2,1,0:T(8,128)}, f32[64,8,128]{2,1,0:T(8,128)S(1)}, u32[]{:S(2)}) copy-start(f32[64,8,128]{2,1,0:T(8,128)S(1)} %all-to-all-done.1.row_parts) | copy-start | bytes 786436
  53.2 51.1 %copy-start.1 = (bf16[4,256,1024]{2,1,0:T(8,128)(2,1)S(1)}, bf16[4,256,1024]{2,1,0:T(8,128)(2,1)}, u32[]{:S(2)}) copy-start(bf16[4,256,1024]{2,1,0:T(8,128)(2,1)} %frames.1) | copy-start | bytes 6291460
  101.4 2.9 %copy-start.4 = (f32[4,256]{1,0:T(4,128)S(1)}, f32[4,256]{1,0:T(4,128)}, u32[]{:S(2)}) copy-start(f32[4,256]{1,0:T(4,128)} %get-tuple-element.8) | copy-start | bytes 12292
  104.1 1.0 copy-start.2
Sparse Core Ops, SparseCore 0:
  10.9 39.0 reduce-scatter.1
  53.3 28.2 all-gather.1

commit v3 on v2

--- a/solution.py
+++ b/solution.py
@@ -85,6 +85,12 @@
     m[HALF:, HALF:] = panel[:, :HALF]
 
 
+def invert(m):
+    @pl.loop(0, 2)
+    def _(step):
+        half_inverse(m)
+
+
 def square_iota():
     return (
         lax.broadcasted_iota(jnp.int32, (HALF, HALF), 0),
@@ -137,7 +143,7 @@
 
 
 def time_kernel(
-    parts, row_parts, diags, time_gram, factor_out, time_out, inverse_out, col_gram
+    parts, row_parts, diags, time_gram, factor_out, time_out, system_out, col_gram, inverse
 ):
     sub = lax.broadcasted_iota(jnp.int32, (8, HALF), 0)
     row_rows, col_rows = [], []
@@ -149,24 +155,24 @@
         col_rows.append(jnp.where(sub < 4, pltpu.roll(even, 4, 0), odd))
     col = unpack_gram(col_rows, diags[1:2, :])
     col_gram[...] = col
-    inverse_out[...] = unpack_gram(row_rows, diags[0:1, :]) * col
+    inverse[...] = unpack_gram(row_rows, diags[0:1, :]) * col
     each = parts.shape[0] // 8
     rhs = [parts[each * i][7:8, :] for i in range(8)]
     rhs = jnp.concatenate(
         [jnp.concatenate(rhs[:4], 0), jnp.concatenate(rhs[4:], 0)], 1
     )
 
-    @pl.loop(0, 4)
-    def _(step):
-        half_inverse(inverse_out)
-
-        @pl.when(step == 1)
-        def _():
-            factor = matmul_f32(rhs, inverse_out[...])
-            factor_out[...] = factor
-            time_new = time_gram[...] + matmul_f32(factor, factor, ((0,), (0,)))
-            time_out[...] = time_new
-            inverse_out[...] = time_new * col_gram[...]
+    invert(inverse)
+    factor = matmul_f32(rhs, inverse[...])
+    factor_out[...] = factor
+    time_new = time_gram[...] + matmul_f32(factor, factor, ((0,), (0,)))
+    time_out[...] = time_new
+    system_out[...] = time_new * col_gram[...]
+
+
+def inverse_kernel(system, inverse):
+    inverse[...] = system[...]
+    invert(inverse)
 
 
 def split_gram(gram):
@@ -174,26 +180,18 @@
     return high, (gram - high.astype(F32)).astype(jnp.bfloat16)
 
 
-def col_kernel(time_new, history, parts, out, inverse, sums):
+def col_kernel(time_new, row_inverse, parts, inverse, gram):
     sub = lax.broadcasted_iota(jnp.int32, (8, R), 0)
-    chunk = history.shape[0] // parts.shape[0]
     for q in range(32):
         rows = []
         for p in (2 * q, 2 * q + 1):
             part = parts[p].astype(F32)
-            sums[chunk * p : chunk * p + chunk, :] = (
-                history[chunk * p : chunk * p + chunk, :] + part[:chunk]
-            )
-            part = part[chunk:]
+            part = part[part.shape[0] - 8 :]
             rows.append(part + pltpu.roll(part, 4, 0))
-        gram = jnp.where(sub < 4, rows[0], rows[1])
-        inverse[8 * q : 8 * q + 8, :] = time_new[8 * q : 8 * q + 8, :] * gram
-
-    @pl.loop(0, 2)
-    def _(step):
-        half_inverse(inverse)
-
-    out[...] = matmul_f32(sums[...], inverse[...]).astype(out.dtype)
+        gram[8 * q : 8 * q + 8, :] = jnp.where(sub < 4, rows[0], rows[1])
+    half = matmul_f32(gram[...], row_inverse[...])
+    inverse[...] = time_new[...] * matmul_f32(row_inverse[...], half)
+    invert(inverse)
 
 
 def gather(x, axis, count):
@@ -234,36 +232,40 @@
     slab_own, message, diags = lax.optimization_barrier((slab_own, message, diags))
     parts = gather(message, "row", nrow)
     slab = lax.all_gather(slab_own, "col", axis=1, tiled=True)
-    frame_factor, time_new, inverse = pl.pallas_call(
+    frame_factor, time_new, system = pl.pallas_call(
         time_kernel,
         out_shape=(jax.ShapeDtypeStruct((nb, R), F32), square, square),
-        scratch_shapes=[pltpu.VMEM((R, R), F32)],
-        name="time_solve",
+        scratch_shapes=[pltpu.VMEM((R, R), F32), pltpu.VMEM((R, R), F32)],
+        name="frame_solve",
     )(parts, row_parts, diags, time_gram)
 
     row_sums = row_history + jnp.sum(frame_factor[:, None, :] * slab, axis=0)
-    new_row = matmul_f32(row_sums, inverse).astype(jnp.bfloat16)
-    high, low = split_gram(inner_gram(new_row))
+    gram_part = matmul_f32(row_sums, row_sums, ((0,), (0,)))
+    gram_part, system = lax.optimization_barrier((gram_part.reshape(nrow, own, R), system))
+    gram_own = lax.all_to_all(gram_part, "row", 0, 0).sum(0)
+    row_inverse = pl.pallas_call(inverse_kernel, out_shape=square, name="row_solve")(system)
+    new_row = matmul_f32(row_sums, row_inverse).astype(jnp.bfloat16)
     products = jnp.einsum("bij,ir->bjr", frames, new_row, preferred_element_type=F32)
     col_part = jnp.sum(frame_factor[:, None, :] * products, axis=0)
     chunk = col_part.shape[0] // nrow
+    halves = jnp.concatenate(split_gram(gram_own), 0)
     message = jnp.concatenate(
         [
             col_part.astype(jnp.bfloat16).reshape(nrow, chunk, R),
-            high.reshape(nrow, own, R),
-            low.reshape(nrow, own, R),
+            jnp.broadcast_to(halves[None], (nrow,) + halves.shape),
         ],
         1,
     )
-    total = lax.all_to_all(message, "row", 0, 0).astype(F32).sum(0)
-    high, low = split_gram(total[chunk : chunk + own] + total[chunk + own :])
-    total = jnp.concatenate([total[:chunk].astype(jnp.bfloat16), high, low], 0)
-    new_col = pl.pallas_call(
+    received = lax.all_to_all(message, "row", 0, 0)
+    total = received[:, :chunk].astype(F32).sum(0).astype(jnp.bfloat16)
+    total = gather(total, "row", nrow).reshape(col_history.shape)
+    col_inverse = pl.pallas_call(
         col_kernel,
-        out_shape=jax.ShapeDtypeStruct(col_history.shape, jnp.bfloat16),
-        scratch_shapes=[pltpu.VMEM((R, R), F32), pltpu.VMEM(col_history.shape, F32)],
+        out_shape=square,
+        scratch_shapes=[pltpu.VMEM((R, R), F32)],
         name="col_solve",
-    )(time_new, col_history, gather(total, "row", nrow))
+    )(time_new, row_inverse, received)
+    new_col = matmul_f32(col_history + total.astype(F32), col_inverse).astype(jnp.bfloat16)
     return (frame_factor, new_row, new_col)
 
 

time: 185 us -> 185 us (level)
  blocking collectives: 84.5 us -> 60.9 us
  starting transfers between devices: 21.5 us -> 32.5 us
  waiting for transfers between devices: 16.5 us -> 23.1 us
  matrix products: 2.32 us -> 5.42 us
    all_to_all x2 -> x1, blocking collectives: 56.1 us -> 25.7 us  [gather(): lax.all_to_all(jnp.broadcast_to(x[None], (count,) + x.shape), axis, 0, 0)]
    pallas_call x1 -> x2, Pallas kernels: 13.2 us -> 24.3 us  [the longest x1 12.9 us: body(): pl.pallas_call(col_kernel, out_shape=square, scratch_shapes=[pltpu.VMEM((...]
    all_to_all x0 -> x2, starting transfers between devices: none -> 11 us  [the longest x1 6.18 us: gather(): lax.all_to_all(jnp.broadcast_to(x[None], (count,) + x.shape), axis, 0, 0)]
    pallas_call x1, Pallas kernels: 22.4 us -> 12.6 us  [body(): pl.pallas_call(time_kernel, out_shape=(jax.ShapeDtypeStruct((nb, R), F32)...]
    all_to_all x1, blocking collectives: 28.4 us -> 35.3 us  [body(): received = lax.all_to_all(message, 'row', 0, 0)]
    all_to_all x0 -> x2, waiting for transfers between devices: none -> 6.6 us  [the longest x1 5.46 us: gather(): lax.all_to_all(jnp.broadcast_to(x[None], (count,) + x.shape), axis, 0, 0)]
    dot_general x1 -> x3, matrix products: 1.33 us -> 4.66 us  [matmul_f32(): lax.dot_general(a, b, (dims, ((), ())), precision=HIGHEST, preferred_elem...]
  transfers between devices with their start and end apart: 4 -> 6, of which waited for: 2 -> 4; matrix products, arithmetic and copies ran while one was open for 1% -> 3% of each run, Pallas kernels for 13% -> 21%
where the time goes in v3:
time: 185 us
  blocking collectives  60.9 us (33%)
  Pallas kernels  42.3 us (23%)
  starting transfers between devices  32.5 us (18%)
  waiting for transfers between devices  23.1 us (12%)
  between operations  14.3 us (8%)
  matrix products  5.42 us (3%)
  other arithmetic  4.12 us (2%)
  local copies, waits for them, and re-layouts  1.92 us (1%)
    all_to_all x1, blocking collectives, body(): received = lax.all_to_all(message, 'row', 0, 0)  35.3 us
    all_to_all x1, blocking collectives, gather(): lax.all_to_all(jnp.broadcast_to(x[None], (count,) + x.shape), axis, 0, 0)  25.7 us
    all_to_all x1, waiting for transfers between devices, body(): row_parts = lax.all_to_all(row_tiles, 'row', 0, 0)  14.8 us
    pallas_call x1, Pallas kernels, body(): pl.pallas_call(col_kernel, out_shape=square, scratch_shapes=[pltpu.VMEM((...  12.9 us
    pallas_call x1, Pallas kernels, body(): pl.pallas_call(time_kernel, out_shape=(jax.ShapeDtypeStruct((nb, R), F32)...  12.6 us
    all_to_all x1, starting transfers between devices, body(): row_parts = lax.all_to_all(row_tiles, 'row', 0, 0)  12.2 us
    pallas_call x1, Pallas kernels, body(): pl.pallas_call(inverse_kernel, out_shape=square, name='row_solve')(system)  11.4 us
    all_to_all x1, starting transfers between devices, body(): col_parts = lax.all_to_all(col_parts, 'col', 0, 0).sum(0)  9.15 us
  transfers between devices with their start and end apart: 6, of which 4 were waited for; matrix products, arithmetic and copies ran while one was open for 3% of the time, Pallas kernels for 21%

profile of v3, /device:TPU:6, one launch (start us, length us, event | category | flops | bytes accessed | tf_op | source)
XLA Modules:
  0.0 184.6 jit_solution(16594145161301304556)
XLA Ops:
  7.2 0.0 reduce-scatter.2.cloned.1.call-start
  7.2 3.6 %local_products.1 = (f32[4,256,256]{2,1,0:T(8,128)}, f32[8,16,128]{2,1,0:T(8,128)}) custom-call(s32[1]{0:T(128)} %bitcast.index, bf16[4,256,1024]{2,1,0:T(8,128)(2,1)} %frames.1, bf16[256,256]{1,0:T(8,128)(2,1)} %factor.1, bf16[1024,256]{1,0:T(8,128)(2,1)} %col_factor.1), custom_call_target="tpu_custom_call" | custom-call | tf_op jit(solution)/shard_map/local_products/pallas_call | solution.py:210
  10.8 9.2 %all-to-all-start = ((f32[8,16,128]{2,1,0:T(8,128)}), f32[8,16,128]{2,1,0:T(8,128)S(1)}, u32[]{:S(2)}, u32[]{:S(2)}) async-start(f32[8,16,128]{2,1,0:T(8,128)} %get-tuple-element.14), calls=%async_computation.1 | async-start | bytes 131072 | tf_op jit(solution)/shard_map/all_to_all | solution.py:221
  20.0 1.8 row_pack.1
  21.8 1.7 all-to-all-done
  23.6 1.8 select_select_fusion
  25.3 12.2 %all-to-all-start.1 = ((f32[64,8,128]{2,1,0:T(8,128)}), f32[64,8,128]{2,1,0:T(8,128)S(1)}, u32[]{:S(2)}, u32[]{:S(2)}) async-start(f32[64,8,128]{2,1,0:T(8,128)} %select_select_fusion), calls=%async_computation.2 | async-start | bytes 524288 | tf_op jit(solution)/shard_map/all_to_all | solution.py:228
  37.6 0.0 all-gather.2.cloned.1.call-start
  37.7 14.8 %all-to-all-done.1.row_parts = f32[64,8,128]{2,1,0:T(8,128)S(1)} async-done(((f32[64,8,128]{2,1,0:T(8,128)}), f32[64,8,128]{2,1,0:T(8,128)S(1)}, u32[]{:S(2)}, u32[]{:S(2)}) %all-to-all-start.1) | async-done | bytes 262176 | tf_op jit(solution)/shard_map/all_to_all | solution.py:228
  52.4 0.1 reduce_sum.58
  52.5 0.6 pad_maximum_fusion.2.diags
  53.2 0.0 all-gather.2.cloned.1.call-update
  53.2 25.7 %all_to_all.30.parts = f32[64,8,128]{2,1,0:T(8,128)} all-to-all(f32[64,8,128]{2,1,0:T(8,128)S(1)} %broadcast_in_dim.48), channel_id=1, replica_groups=mesh['row'=64,'col'=8] {'row'}, dimensions={0} | all-to-all | bytes 524288 | tf_op jit(solution)/shard_map/all_to_all | solution.py:198
  78.9 12.6 %frame_solve.1 = (f32[4,256]{1,0:T(4,128)}, f32[256,256]{1,0:T(8,128)}, f32[256,256]{1,0:T(8,128)}) custom-call(f32[64,8,128]{2,1,0:T(8,128)} %all_to_all.30.parts, f32[64,8,128]{2,1,0:T(8,128)} %copy-done.1, f32[8,128]{1,0:T(8,128)} %pad_maximum_fusion.2.diags, f32[256,256]{1,0:T(8,128)} %time_gram.1), custom_call_target="tpu_custom_call" | custom-call | tf_op jit(solution)/shard_map/frame_solve/pallas_call | solution.py:235
  91.5 1.3 multiply_reduce_fusion
  92.9 0.6 fusion.4
  93.5 0.8 reshape.25
  94.3 4.8 %all-to-all-start.3 = ((f32[64,4,256]{2,1,0:T(4,128)}), f32[64,4,256]{2,1,0:T(4,128)S(1)}, u32[]{:S(2)}, u32[]{:S(2)}) async-start(f32[64,4,256]{2,1,0:T(4,128)} %reshape.25), calls=%async_computation.4 | async-start | bytes 524288 | tf_op jit(solution)/shard_map/all_to_all | solution.py:245
  99.1 11.4 %row_solve.1.row_inverse = f32[256,256]{1,0:T(8,128)} custom-call(f32[256,256]{1,0:T(8,128)} %get-tuple-element.20.system), custom_call_target="tpu_custom_call" | custom-call | tf_op jit(solution)/shard_map/row_solve/pallas_call | solution.py:246
  110.5 1.3 convolution_convert_fusion.1
  111.9 0.8 fusion
  112.7 0.2 copy.11
  112.9 1.1 all-to-all-done.3
  114.1 0.1 reduce_sum.61
  114.2 0.1 pad_maximum_fusion
  114.2 35.3 %all_to_all.31.parts = bf16[64,24,256]{2,1,0:T(8,128)(2,1)S(1)} all-to-all(bf16[64,24,256]{2,1,0:T(8,128)(2,1)S(1)} %pad_maximum_fusion), channel_id=1, replica_groups=mesh['row'=64,'col'=8] {'row'}, dimensions={0} | all-to-all | bytes 1572864 | tf_op jit(solution)/shard_map/all_to_all | solution.py:259
  149.5 0.1 slice_reduce_fusion
  149.6 0.8 broadcast_in_dim.50
  150.5 6.2 %all-to-all-start.5 = ((bf16[64,16,256]{2,1,0:T(8,128)(2,1)}), bf16[64,16,256]{2,1,0:T(8,128)(2,1)S(1)}, u32[]{:S(2)}, u32[]{:S(2)}) async-start(bf16[64,16,256]{2,1,0:T(8,128)(2,1)} %broadcast_in_dim.50), calls=%async_computation.6 | async-start | bytes 1048576 | tf_op jit(solution)/shard_map/all_to_all | solution.py:198
  156.7 12.9 %col_solve.1 = f32[256,256]{1,0:T(8,128)} custom-call(f32[256,256]{1,0:T(8,128)} %get-tuple-element.22.time_new, f32[256,256]{1,0:T(8,128)} %row_solve.1.row_inverse, bf16[64,24,256]{2,1,0:T(8,128)(2,1)} %copy-done), custom_call_target="tpu_custom_call" | custom-call | tf_op jit(solution)/shard_map/col_solve/pallas_call | solution.py:262
  169.5 5.5 %all-to-all-done.5 = bf16[64,16,256]{2,1,0:T(8,128)(2,1)S(1)} async-done(((bf16[64,16,256]{2,1,0:T(8,128)(2,1)}), bf16[64,16,256]{2,1,0:T(8,128)(2,1)S(1)}, u32[]{:S(2)}, u32[]{:S(2)}) %all-to-all-start.5) | async-done | bytes 524320 | tf_op jit(solution)/shard_map/all_to_all | solution.py:198
  175.0 2.7 %convolution_convert_fusion = bf16[1024,256]{1,0:T(8,128)(2,1)} fusion(f32[256,256]{1,0:T(8,128)} %col_solve.1, f32[1024,256]{1,0:T(8,128)S(1)} %copy-done.3, bf16[1024,256]{1,0:T(8,128)(2,1)S(1)} %bitcast.22), kind=kOutput, calls=%fused_computation.2 | convolution fusion | flops 806092800 | bytes 2359296 | tf_op jit(solution)/shard_map/dot_general | solution.py:21
  (32 shorter events, 0.2 us)
Async XLA Ops:
  7.2 46.0 %reduce-scatter.2.cloned.1.call-start = ((), (), s32[]{:S(2)}) async-start(), calls=%async_computation.7 | async-start | bytes 1179648 | tf_op jit(solution)/shard_map/reduce_scatter | solution.py:220
  10.8 12.7 %all-to-all-start = ((f32[8,16,128]{2,1,0:T(8,128)}), f32[8,16,128]{2,1,0:T(8,128)S(1)}, u32[]{:S(2)}, u32[]{:S(2)}) async-start(f32[8,16,128]{2,1,0:T(8,128)} %get-tuple-element.14), calls=%async_computation.1 | async-start | bytes 131072 | tf_op jit(solution)/shard_map/all_to_all | solution.py:221
  23.5 69.3 %copy-start.4 = (f32[256,256]{1,0:T(8,128)S(1)}, f32[256,256]{1,0:T(8,128)}, u32[]{:S(2)}) copy-start(f32[256,256]{1,0:T(8,128)} %param.9) | copy-start | bytes 786436
  25.3 27.1 %all-to-all-start.1 = ((f32[64,8,128]{2,1,0:T(8,128)}), f32[64,8,128]{2,1,0:T(8,128)S(1)}, u32[]{:S(2)}, u32[]{:S(2)}) async-start(f32[64,8,128]{2,1,0:T(8,128)} %select_select_fusion), calls=%async_computation.2 | async-start | bytes 524288 | tf_op jit(solution)/shard_map/all_to_all | solution.py:228
  37.6 53.9 %all-gather.2.cloned.1.call-start = ((), (), s32[]{:S(2)}) async-start(), calls=%async_computation.8 | async-start | bytes 1179648 | tf_op jit(solution)/shard_map/all_gather | solution.py:234
  52.4 26.4 %copy-start.1 = (f32[64,8,128]{2,1,0:T(8,128)}, f32[64,8,128]{2,1,0:T(8,128)S(1)}, u32[]{:S(2)}) copy-start(f32[64,8,128]{2,1,0:T(8,128)S(1)} %all-to-all-done.1.row_parts) | copy-start | bytes 786436
  92.8 19.0 %copy-start.2 = (bf16[4,256,1024]{2,1,0:T(8,128)(2,1)S(1)}, bf16[4,256,1024]{2,1,0:T(8,128)(2,1)}, u32[]{:S(2)}) copy-start(bf16[4,256,1024]{2,1,0:T(8,128)(2,1)} %frames.1) | copy-start | bytes 6291460
  92.9 19.0 %copy-start.6 = (f32[4,256]{1,0:T(4,128)S(1)}, f32[4,256]{1,0:T(4,128)}, u32[]{:S(2)}) copy-start(f32[4,256]{1,0:T(4,128)} %get-tuple-element.10) | copy-start | bytes 12292
  94.3 19.8 %all-to-all-start.3 = ((f32[64,4,256]{2,1,0:T(4,128)}), f32[64,4,256]{2,1,0:T(4,128)S(1)}, u32[]{:S(2)}, u32[]{:S(2)}) async-start(f32[64,4,256]{2,1,0:T(4,128)} %reshape.25), calls=%async_computation.4 | async-start | bytes 524288 | tf_op jit(solution)/shard_map/all_to_all | solution.py:245
  111.9 1.0 copy-start.5
  149.5 7.1 %copy-start = (bf16[64,24,256]{2,1,0:T(8,128)(2,1)}, bf16[64,24,256]{2,1,0:T(8,128)(2,1)S(1)}, u32[]{:S(2)}) copy-start(bf16[64,24,256]{2,1,0:T(8,128)(2,1)S(1)} %all_to_all.31.parts) | copy-start | bytes 2359300
  149.5 25.5 %copy-start.3 = (f32[1024,256]{1,0:T(8,128)S(1)}, f32[1024,256]{1,0:T(8,128)}, u32[]{:S(2)}) copy-start(f32[1024,256]{1,0:T(8,128)} %param.10) | copy-start | bytes 3145732
  150.5 24.5 %all-to-all-start.5 = ((bf16[64,16,256]{2,1,0:T(8,128)(2,1)}), bf16[64,16,256]{2,1,0:T(8,128)(2,1)S(1)}, u32[]{:S(2)}, u32[]{:S(2)}) async-start(bf16[64,16,256]{2,1,0:T(8,128)(2,1)} %broadcast_in_dim.50), calls=%async_computation.6 | async-start | bytes 1048576 | tf_op jit(solution)/shard_map/all_to_all | solution.py:198
Sparse Core Ops, SparseCore 0:
  10.9 39.0 reduce-scatter.1
  53.3 28.2 all-gather.1

commit v4 on v2

--- a/solution.py
+++ b/solution.py
@@ -69,9 +69,10 @@
                 jnp.broadcast_to(tiles[i][:, g + j : g + j + 1], (8, R)) * rows[j]
                 for j in range(8)
             ]
-            while len(acc) > 1:
-                acc = [acc[k] + acc[k + 1] for k in range(0, len(acc), 2)]
-            tiles[i] = jnp.where(inside, 0.0, tiles[i]) - acc[0]
+            new = jnp.where(inside, 0.0, tiles[i])
+            for term in acc:
+                new = new - term
+            tiles[i] = new
         merged = rows[0]
         for j in range(1, 8):
             merged = jnp.where(sub8 == j, rows[j], merged)
@@ -174,16 +175,16 @@
     return high, (gram - high.astype(F32)).astype(jnp.bfloat16)
 
 
-def col_kernel(time_new, history, parts, out, inverse, sums):
+def col_kernel(time_new, history, parts, out, inverse, sums, past, loaded):
     sub = lax.broadcasted_iota(jnp.int32, (8, R), 0)
     chunk = history.shape[0] // parts.shape[0]
+    load = pltpu.make_async_copy(history, past, loaded)
+    load.start()
     for q in range(32):
         rows = []
         for p in (2 * q, 2 * q + 1):
             part = parts[p].astype(F32)
-            sums[chunk * p : chunk * p + chunk, :] = (
-                history[chunk * p : chunk * p + chunk, :] + part[:chunk]
-            )
+            sums[chunk * p : chunk * p + chunk, :] = part[:chunk]
             part = part[chunk:]
             rows.append(part + pltpu.roll(part, 4, 0))
         gram = jnp.where(sub < 4, rows[0], rows[1])
@@ -193,7 +194,8 @@
     def _(step):
         half_inverse(inverse)
 
-    out[...] = matmul_f32(sums[...], inverse[...]).astype(out.dtype)
+    load.wait()
+    out[...] = matmul_f32(past[...] + sums[...], inverse[...]).astype(out.dtype)
 
 
 def gather(x, axis, count):
@@ -227,10 +229,12 @@
     row_tiles = jnp.where(
         sub < 5, row_tiles, jnp.where(sub == 5, col_parts[3][None, None], rhs_rows)
     )
+    col_share, col_diag = col_parts[:3], col_parts[4:5]
+    row_tiles, col_share, col_diag = lax.optimization_barrier((row_tiles, col_share, col_diag))
     row_parts = lax.all_to_all(row_tiles, "row", 0, 0)
     row_own = row_parts.sum(0)
-    message = jnp.concatenate([row_own[:4], col_parts[:3], row_own[6:7]], 0)
-    diags = jnp.concatenate([row_own[4:5], col_parts[4:5], row_own[2:8]], 0)
+    message = jnp.concatenate([row_own[:4], col_share, row_own[6:7]], 0)
+    diags = jnp.concatenate([row_own[4:5], col_diag, row_own[2:8]], 0)
     slab_own, message, diags = lax.optimization_barrier((slab_own, message, diags))
     parts = gather(message, "row", nrow)
     slab = lax.all_gather(slab_own, "col", axis=1, tiled=True)
@@ -261,7 +265,13 @@
     new_col = pl.pallas_call(
         col_kernel,
         out_shape=jax.ShapeDtypeStruct(col_history.shape, jnp.bfloat16),
-        scratch_shapes=[pltpu.VMEM((R, R), F32), pltpu.VMEM(col_history.shape, F32)],
+        in_specs=[vmem, pl.BlockSpec(memory_space=pl.ANY), vmem],
+        scratch_shapes=[
+            pltpu.VMEM((R, R), F32),
+            pltpu.VMEM(col_history.shape, F32),
+            pltpu.VMEM(col_history.shape, F32),
+            pltpu.SemaphoreType.DMA,
+        ],
         name="col_solve",
     )(time_new, col_history, gather(total, "row", nrow))
     return (frame_factor, new_row, new_col)

time: 185 us -> 184 us (level)
  blocking collectives: 84.5 us -> 112 us
  waiting for transfers between devices: 16.5 us -> 1.72 us
  starting transfers between devices: 21.5 us -> 9.19 us
    all_to_all x0 -> x1, blocking collectives: none -> 26.9 us  [body(): row_parts = lax.all_to_all(row_tiles, 'row', 0, 0)]
    all_to_all x1 -> x0, waiting for transfers between devices: 14.8 us -> none  [body(): row_parts = lax.all_to_all(row_tiles, 'row', 0, 0)]
    all_to_all x1 -> x0, starting transfers between devices: 12.2 us -> none  [body(): row_parts = lax.all_to_all(row_tiles, 'row', 0, 0)]
  transfers between devices with their start and end apart: 4 -> 3, of which waited for: 2 -> 1; matrix products, arithmetic and copies ran while one was open for 1% -> 1% of each run, Pallas kernels for 13% -> 13%
where the time goes in v4:
time: 184 us; the launch traced here: 183 us
  blocking collectives  112 us (61%)
  Pallas kernels  40.2 us (22%)
  between operations  14.2 us (8%)
  starting transfers between devices  9.19 us (5%)
  other arithmetic  3.47 us (2%)
  matrix products  2.32 us (1%)
    all_to_all x2, blocking collectives, gather(): lax.all_to_all(jnp.broadcast_to(x[None], (count,) + x.shape), axis, 0, 0)  56.5 us
    all_to_all x1, blocking collectives, body(): total = lax.all_to_all(message, 'row', 0, 0).astype(F32).sum(0)  28.4 us
    all_to_all x1, blocking collectives, body(): row_parts = lax.all_to_all(row_tiles, 'row', 0, 0)  26.9 us
    pallas_call x1, Pallas kernels, body(): pl.pallas_call(time_kernel, out_shape=(jax.ShapeDtypeStruct((nb, R), F32)...  22.1 us
    pallas_call x1, Pallas kernels, body(): pl.pallas_call(col_kernel, out_shape=jax.ShapeDtypeStruct(col_history.sha...  12.7 us
    all_to_all x1, starting transfers between devices, body(): col_parts = lax.all_to_all(col_parts, 'col', 0, 0).sum(0)  9.15 us
  transfers between devices with their start and end apart: 3, of which 1 were waited for; matrix products, arithmetic and copies ran while one was open for 1% of the time, Pallas kernels for 13%

profile of v4, /device:TPU:6, one launch (start us, length us, event | category | flops | bytes accessed | tf_op | source)
XLA Modules:
  0.0 183.3 jit_solution(12084373414434125828)
XLA Ops:
  7.2 0.0 reduce-scatter.2.cloned.1.call-start
  7.2 3.6 %local_products.1 = (f32[4,256,256]{2,1,0:T(8,128)}, f32[8,16,128]{2,1,0:T(8,128)}) custom-call(s32[1]{0:T(128)} %bitcast.index, bf16[4,256,1024]{2,1,0:T(8,128)(2,1)} %frames.1, bf16[256,256]{1,0:T(8,128)(2,1)} %factor.1, bf16[1024,256]{1,0:T(8,128)(2,1)} %col_factor.1), custom_call_target="tpu_custom_call" | custom-call | tf_op jit(solution)/shard_map/local_products/pallas_call | solution.py:214
  10.8 0.0 reduce-scatter.2.cloned.1.call-update
  10.8 9.2 %all-to-all-start = ((f32[8,16,128]{2,1,0:T(8,128)}), f32[8,16,128]{2,1,0:T(8,128)S(1)}, u32[]{:S(2)}, u32[]{:S(2)}) async-start(f32[8,16,128]{2,1,0:T(8,128)} %get-tuple-element.15), calls=%async_computation.1 | async-start | bytes 131072 | tf_op jit(solution)/shard_map/all_to_all | solution.py:225
  20.0 0.0 all-gather.2.cloned.1.call-start
  20.0 1.8 %row_pack.1 = f32[64,8,128]{2,1,0:T(8,128)} custom-call(bf16[256,256]{1,0:T(8,128)(2,1)} %factor.1), custom_call_target="tpu_custom_call" | custom-call | tf_op jit(solution)/shard_map/row_pack/pallas_call | solution.py:226
  21.8 1.7 all-to-all-done
  23.5 0.0 copy-start.3
  23.6 1.1 select_select_fusion
  24.7 26.9 %all_to_all.25.row_parts = f32[64,8,128]{2,1,0:T(8,128)S(1)} all-to-all(f32[64,8,128]{2,1,0:T(8,128)S(1)} %select_select_fusion), channel_id=1, replica_groups=mesh['row'=64,'col'=8] {'row'}, dimensions={0} | all-to-all | bytes 524288 | tf_op jit(solution)/shard_map/all_to_all | solution.py:234
  51.5 0.1 reduce_sum.46
  51.6 0.6 pad_maximum_fusion.3.diags
  52.3 0.0 all-gather.2.cloned.1.call-update
  52.3 0.0 copy-start.1
  52.3 26.7 %all_to_all.26.parts = f32[64,8,128]{2,1,0:T(8,128)} all-to-all(f32[64,8,128]{2,1,0:T(8,128)S(1)} %broadcast_in_dim.42), channel_id=1, replica_groups=mesh['row'=64,'col'=8] {'row'}, dimensions={0} | all-to-all | bytes 524288 | tf_op jit(solution)/shard_map/all_to_all | solution.py:202
  79.0 0.0 copy-done
  79.0 22.1 %time_solve.1 = (f32[4,256]{1,0:T(4,128)}, f32[256,256]{1,0:T(8,128)}, f32[256,256]{1,0:T(8,128)}) custom-call(f32[64,8,128]{2,1,0:T(8,128)} %all_to_all.26.parts, f32[64,8,128]{2,1,0:T(8,128)} %copy-done, f32[8,128]{1,0:T(8,128)} %pad_maximum_fusion.3.diags, f32[256,256]{1,0:T(8,128)} %time_gram.1), custom_call_target="tpu_custom_call" | custom-call | tf_op jit(solution)/shard_map/time_solve/pallas_call | solution.py:241
  101.1 1.3 multiply_reduce_fusion
  102.4 0.0 copy-done.3
  102.4 1.3 convolution_convert_fusion
  103.7 0.0 copy-start.2
  103.7 0.2 subtract_convert_fusion
  104.0 0.0 copy-done.1
  104.0 0.8 fusion
  104.8 0.0 copy-done.2
  104.9 0.2 copy.14
  105.1 0.2 pad_maximum_fusion
  105.3 28.4 %all_to_all.27 = bf16[64,24,256]{2,1,0:T(8,128)(2,1)S(1)} all-to-all(bf16[64,24,256]{2,1,0:T(8,128)(2,1)S(1)} %pad_maximum_fusion), channel_id=1, replica_groups=mesh['row'=64,'col'=8] {'row'}, dimensions={0} | all-to-all | bytes 1572864 | tf_op jit(solution)/shard_map/all_to_all | solution.py:262
  133.7 0.1 convert_reduce_fusion
  133.9 0.1 broadcast_in_dim.43
  133.9 29.9 %all_to_all.28.parts = bf16[64,24,256]{2,1,0:T(8,128)(2,1)} all-to-all(bf16[64,24,256]{2,1,0:T(8,128)(2,1)S(1)} %broadcast_in_dim.43), channel_id=1, replica_groups=mesh['row'=64,'col'=8] {'row'}, dimensions={0} | all-to-all | bytes 1572864 | tf_op jit(solution)/shard_map/all_to_all | solution.py:202
  163.8 12.7 %col_solve.1 = bf16[1024,256]{1,0:T(8,128)(2,1)} custom-call(f32[256,256]{1,0:T(8,128)} %get-tuple-element.24.time_new, f32[1024,256]{1,0:T(8,128)} %history.1, bf16[64,24,256]{2,1,0:T(8,128)(2,1)} %all_to_all.28.parts), custom_call_target="tpu_custom_call" | custom-call | tf_op jit(solution)/shard_map/col_solve/pallas_call | solution.py:265
  (21 shorter events, 0.2 us)
Async XLA Ops:
  7.2 45.1 %reduce-scatter.2.cloned.1.call-start = ((), (), s32[]{:S(2)}) async-start(), calls=%async_computation.6 | async-start | bytes 1179648 | tf_op jit(solution)/shard_map/reduce_scatter | solution.py:224
  10.8 12.7 %all-to-all-start = ((f32[8,16,128]{2,1,0:T(8,128)}), f32[8,16,128]{2,1,0:T(8,128)S(1)}, u32[]{:S(2)}, u32[]{:S(2)}) async-start(f32[8,16,128]{2,1,0:T(8,128)} %get-tuple-element.15), calls=%async_computation.1 | async-start | bytes 131072 | tf_op jit(solution)/shard_map/all_to_all | solution.py:225
  20.0 81.1 %all-gather.2.cloned.1.call-start = ((), (), s32[]{:S(2)}) async-start(), calls=%async_computation.7 | async-start | bytes 1179648 | tf_op jit(solution)/shard_map/all_gather | solution.py:240
  23.5 78.8 %copy-start.3 = (f32[256,256]{1,0:T(8,128)S(1)}, f32[256,256]{1,0:T(8,128)}, u32[]{:S(2)}) copy-start(f32[256,256]{1,0:T(8,128)} %param.9) | copy-start | bytes 786436
  51.5 27.4 %copy-start = (f32[64,8,128]{2,1,0:T(8,128)}, f32[64,8,128]{2,1,0:T(8,128)S(1)}, u32[]{:S(2)}) copy-start(f32[64,8,128]{2,1,0:T(8,128)S(1)} %all_to_all.25.row_parts) | copy-start | bytes 786436
  52.3 51.7 %copy-start.1 = (bf16[4,256,1024]{2,1,0:T(8,128)(2,1)S(1)}, bf16[4,256,1024]{2,1,0:T(8,128)(2,1)}, u32[]{:S(2)}) copy-start(bf16[4,256,1024]{2,1,0:T(8,128)(2,1)} %frames.1) | copy-start | bytes 6291460
  101.0 2.9 %copy-start.4 = (f32[4,256]{1,0:T(4,128)S(1)}, f32[4,256]{1,0:T(4,128)}, u32[]{:S(2)}) copy-start(f32[4,256]{1,0:T(4,128)} %get-tuple-element.11) | copy-start | bytes 12292
  103.7 1.0 copy-start.2
Sparse Core Ops, SparseCore 0:
  10.9 39.0 reduce-scatter.1
  52.4 29.2 all-gather.1

commit v5 on v4

--- a/solution.py
+++ b/solution.py
@@ -118,19 +118,22 @@
     )
 
 
-def local_kernel(index, frames, row_factor, col_factor, slab_out, message, tiles):
+def slab_kernel(frames, row_factor, col_factor, slab_out, sums_out):
     rows = row_factor[...].astype(F32)
-    sums = []
     for b in range(frames.shape[0]):
         slab = jnp.dot(frames[b], col_factor[...], preferred_element_type=F32)
         slab_out[b] = slab
-        sums.append(jnp.sum(slab * rows, 0, keepdims=True))
+        total = jnp.sum(slab * rows, 0, keepdims=True)
+        sums_out[b : b + 1, :] = total[:, :HALF]
+        sums_out[b + 4 : b + 5, :] = total[:, HALF:]
+
+
+def col_message_kernel(index, col_factor, sums, message, tiles):
     pack_gram(inner_gram(col_factor[...]), tiles)
     own = tiles[index[0]]
-    sums = jnp.concatenate([x[:, :HALF] for x in sums] + [x[:, HALF:] for x in sums], 0)
     for i in range(message.shape[0]):
         message[i, :8] = own
-        message[i, 8:] = sums
+        message[i, 8:] = sums[...]
 
 
 def row_pack_kernel(factor, out):
@@ -211,16 +214,21 @@
     square = jax.ShapeDtypeStruct((R, R), F32)
     tiles = jax.ShapeDtypeStruct((nrow, 8, HALF), F32)
     vmem = pl.BlockSpec(memory_space=pltpu.VMEM)
-    slab_part, col_parts = pl.pallas_call(
-        local_kernel,
+    slab_part, rhs_part = pl.pallas_call(
+        slab_kernel,
         out_shape=(
             jax.ShapeDtypeStruct((nb,) + row_history.shape, F32),
-            jax.ShapeDtypeStruct((ncol, 16, HALF), F32),
+            jax.ShapeDtypeStruct((8, HALF), F32),
         ),
-        in_specs=[pl.BlockSpec(memory_space=pltpu.SMEM), vmem, vmem, vmem],
+        name="slab_products",
+    )(frames, row_factor, col_factor)
+    col_parts = pl.pallas_call(
+        col_message_kernel,
+        out_shape=jax.ShapeDtypeStruct((ncol, 16, HALF), F32),
+        in_specs=[pl.BlockSpec(memory_space=pltpu.SMEM), vmem, vmem],
         scratch_shapes=[pltpu.VMEM(tiles.shape, F32)],
-        name="local_products",
-    )(r.reshape(1), frames, row_factor, col_factor)
+        name="col_message",
+    )(r.reshape(1), col_factor, rhs_part)
     slab_own = lax.psum_scatter(slab_part, "col", scatter_dimension=1, tiled=True)
     col_parts = lax.all_to_all(col_parts, "col", 0, 0).sum(0)
     row_tiles = pl.pallas_call(row_pack_kernel, out_shape=tiles, name="row_pack")(row_factor)

time: 184 us -> 184 us (level)
  blocking collectives: 112 us -> 110 us
  Pallas kernels: 40.2 us -> 42.1 us
    all_to_all x2, blocking collectives: 56.5 us -> 54.5 us  [gather(): lax.all_to_all(jnp.broadcast_to(x[None], (count,) + x.shape), axis, 0, 0)]
    pallas_call x1 -> x2, Pallas kernels: 3.57 us -> 5.48 us  [the longest x1 3.43 us: body(): pl.pallas_call(slab_kernel, out_shape=(jax.ShapeDtypeStruct((nb,) + row_h...]
  transfers between devices with their start and end apart: 3 -> 3, of which waited for: 1 -> 1; matrix products, arithmetic and copies ran while one was open for 1% -> 1% of each run, Pallas kernels for 13% -> 14%
where the time goes in v5:
time: 184 us
  blocking collectives  110 us (60%)
  Pallas kernels  42.1 us (23%)
  between operations  14.2 us (8%)
  starting transfers between devices  9.18 us (5%)
  other arithmetic  3.47 us (2%)
  matrix products  2.32 us (1%)
    all_to_all x2, blocking collectives, gather(): lax.all_to_all(jnp.broadcast_to(x[None], (count,) + x.shape), axis, 0, 0)  54.5 us
    all_to_all x1, blocking collectives, body(): total = lax.all_to_all(message, 'row', 0, 0).astype(F32).sum(0)  28.9 us
    all_to_all x1, blocking collectives, body(): row_parts = lax.all_to_all(row_tiles, 'row', 0, 0)  26.9 us
    pallas_call x1, Pallas kernels, body(): pl.pallas_call(time_kernel, out_shape=(jax.ShapeDtypeStruct((nb, R), F32)...  22.1 us
    pallas_call x1, Pallas kernels, body(): pl.pallas_call(col_kernel, out_shape=jax.ShapeDtypeStruct(col_history.sha...  12.7 us
    all_to_all x1, starting transfers between devices, body(): col_parts = lax.all_to_all(col_parts, 'col', 0, 0).sum(0)  9.14 us
  transfers between devices with their start and end apart: 3, of which 1 were waited for; matrix products, arithmetic and copies ran while one was open for 1% of the time, Pallas kernels for 14%

profile of v5, /device:TPU:6, one launch (start us, length us, event | category | flops | bytes accessed | tf_op | source)
XLA Modules:
  0.0 183.7 jit_solution(8417891184140536707)
XLA Ops:
  7.2 0.0 reduce-scatter.2.cloned.1.call-start
  7.2 3.4 %slab_products.1 = (f32[4,256,256]{2,1,0:T(8,128)}, f32[8,128]{1,0:T(8,128)}) custom-call(bf16[4,256,1024]{2,1,0:T(8,128)(2,1)} %frames.1, bf16[256,256]{1,0:T(8,128)(2,1)} %factor.1, bf16[1024,256]{1,0:T(8,128)(2,1)} %col_factor.3), custom_call_target="tpu_custom_call" | custom-call | tf_op jit(solution)/shard_map/slab_products/pallas_call | solution.py:217
  10.6 0.0 reduce-scatter.2.cloned.1.call-update
  10.7 2.1 %col_message.1 = f32[8,16,128]{2,1,0:T(8,128)} custom-call(s32[1]{0:T(128)} %bitcast.index, bf16[1024,256]{1,0:T(8,128)(2,1)} %col_factor.3, f32[8,128]{1,0:T(8,128)} %get-tuple-element.15.sums), custom_call_target="tpu_custom_call" | custom-call | tf_op jit(solution)/shard_map/col_message/pallas_call | solution.py:225
  12.7 9.1 %all-to-all-start = ((f32[8,16,128]{2,1,0:T(8,128)}), f32[8,16,128]{2,1,0:T(8,128)S(1)}, u32[]{:S(2)}, u32[]{:S(2)}) async-start(f32[8,16,128]{2,1,0:T(8,128)} %col_message.1), calls=%async_computation.1 | async-start | bytes 131072 | tf_op jit(solution)/shard_map/all_to_all | solution.py:233
  21.9 0.0 all-gather.2.cloned.1.call-start
  21.9 1.8 %row_pack.1 = f32[64,8,128]{2,1,0:T(8,128)} custom-call(bf16[256,256]{1,0:T(8,128)(2,1)} %factor.1), custom_call_target="tpu_custom_call" | custom-call | tf_op jit(solution)/shard_map/row_pack/pallas_call | solution.py:234
  23.7 1.7 all-to-all-done
  25.5 0.0 copy-start.3
  25.5 1.1 select_select_fusion
  26.6 26.9 %all_to_all.25.row_parts = f32[64,8,128]{2,1,0:T(8,128)S(1)} all-to-all(f32[64,8,128]{2,1,0:T(8,128)S(1)} %select_select_fusion), channel_id=1, replica_groups=mesh['row'=64,'col'=8] {'row'}, dimensions={0} | all-to-all | bytes 524288 | tf_op jit(solution)/shard_map/all_to_all | solution.py:242
  53.4 0.1 reduce_sum.46
  53.6 0.6 pad_maximum_fusion.3.diags
  54.2 0.0 all-gather.2.cloned.1.call-update
  54.2 0.0 copy-start.1
  54.2 24.2 %all_to_all.26.parts = f32[64,8,128]{2,1,0:T(8,128)} all-to-all(f32[64,8,128]{2,1,0:T(8,128)S(1)} %broadcast_in_dim.42), channel_id=1, replica_groups=mesh['row'=64,'col'=8] {'row'}, dimensions={0} | all-to-all | bytes 524288 | tf_op jit(solution)/shard_map/all_to_all | solution.py:205
  78.4 0.0 copy-done
  78.4 22.1 %time_solve.1 = (f32[4,256]{1,0:T(4,128)}, f32[256,256]{1,0:T(8,128)}, f32[256,256]{1,0:T(8,128)}) custom-call(f32[64,8,128]{2,1,0:T(8,128)} %all_to_all.26.parts, f32[64,8,128]{2,1,0:T(8,128)} %copy-done, f32[8,128]{1,0:T(8,128)} %pad_maximum_fusion.3.diags, f32[256,256]{1,0:T(8,128)} %time_gram.1), custom_call_target="tpu_custom_call" | custom-call | tf_op jit(solution)/shard_map/time_solve/pallas_call | solution.py:249
  100.5 1.3 multiply_reduce_fusion
  101.8 0.0 copy-done.3
  101.8 1.3 convolution_convert_fusion
  103.2 0.0 copy-start.2
  103.2 0.2 subtract_convert_fusion
  103.4 0.0 copy-done.1
  103.5 0.8 fusion
  104.3 0.2 copy.14
  104.5 0.2 pad_maximum_fusion
  104.7 28.9 %all_to_all.27 = bf16[64,24,256]{2,1,0:T(8,128)(2,1)S(1)} all-to-all(bf16[64,24,256]{2,1,0:T(8,128)(2,1)S(1)} %pad_maximum_fusion), channel_id=1, replica_groups=mesh['row'=64,'col'=8] {'row'}, dimensions={0} | all-to-all | bytes 1572864 | tf_op jit(solution)/shard_map/all_to_all | solution.py:270
  133.6 0.1 convert_reduce_fusion
  133.8 0.1 broadcast_in_dim.43
  133.8 30.3 %all_to_all.28.parts = bf16[64,24,256]{2,1,0:T(8,128)(2,1)} all-to-all(bf16[64,24,256]{2,1,0:T(8,128)(2,1)S(1)} %broadcast_in_dim.43), channel_id=1, replica_groups=mesh['row'=64,'col'=8] {'row'}, dimensions={0} | all-to-all | bytes 1572864 | tf_op jit(solution)/shard_map/all_to_all | solution.py:205
  164.1 12.7 %col_solve.1 = bf16[1024,256]{1,0:T(8,128)(2,1)} custom-call(f32[256,256]{1,0:T(8,128)} %get-tuple-element.24.time_new, f32[1024,256]{1,0:T(8,128)} %history.1, bf16[64,24,256]{2,1,0:T(8,128)(2,1)} %all_to_all.28.parts), custom_call_target="tpu_custom_call" | custom-call | tf_op jit(solution)/shard_map/col_solve/pallas_call | solution.py:273
  (22 shorter events, 0.2 us)
Async XLA Ops:
  7.2 47.0 %reduce-scatter.2.cloned.1.call-start = ((), (), s32[]{:S(2)}) async-start(), calls=%async_computation.6 | async-start | bytes 1179648 | tf_op jit(solution)/shard_map/reduce_scatter | solution.py:232
  12.7 12.7 %all-to-all-start = ((f32[8,16,128]{2,1,0:T(8,128)}), f32[8,16,128]{2,1,0:T(8,128)S(1)}, u32[]{:S(2)}, u32[]{:S(2)}) async-start(f32[8,16,128]{2,1,0:T(8,128)} %col_message.1), calls=%async_computation.1 | async-start | bytes 131072 | tf_op jit(solution)/shard_map/all_to_all | solution.py:233
  21.9 78.6 %all-gather.2.cloned.1.call-start = ((), (), s32[]{:S(2)}) async-start(), calls=%async_computation.7 | async-start | bytes 1179648 | tf_op jit(solution)/shard_map/all_gather | solution.py:248
  25.5 76.4 %copy-start.3 = (f32[256,256]{1,0:T(8,128)S(1)}, f32[256,256]{1,0:T(8,128)}, u32[]{:S(2)}) copy-start(f32[256,256]{1,0:T(8,128)} %param.9) | copy-start | bytes 786436
  53.4 25.0 %copy-start = (f32[64,8,128]{2,1,0:T(8,128)}, f32[64,8,128]{2,1,0:T(8,128)S(1)}, u32[]{:S(2)}) copy-start(f32[64,8,128]{2,1,0:T(8,128)S(1)} %all_to_all.25.row_parts) | copy-start | bytes 786436
  54.2 49.2 %copy-start.1 = (bf16[4,256,1024]{2,1,0:T(8,128)(2,1)S(1)}, bf16[4,256,1024]{2,1,0:T(8,128)(2,1)}, u32[]{:S(2)}) copy-start(bf16[4,256,1024]{2,1,0:T(8,128)(2,1)} %frames.1) | copy-start | bytes 6291460
  100.5 2.9 %copy-start.4 = (f32[4,256]{1,0:T(4,128)S(1)}, f32[4,256]{1,0:T(4,128)}, u32[]{:S(2)}) copy-start(f32[4,256]{1,0:T(4,128)} %get-tuple-element.11) | copy-start | bytes 12292
  103.2 1.0 copy-start.2
Sparse Core Ops, SparseCore 0:
  10.8 38.9 reduce-scatter.1
  54.3 27.1 all-gather.1
